TPU v7x, 32 devices: a whole 2x2x4 slice. The times are simulated.
32 devices in a mesh: grp: 2 (over x), date: 8 (over z, y), pix: 2 (over core).
Axes of the slice: x: 2, y: 2, z: 4, core: 2. Of those that a mesh axis runs over, the one named last changes fastest.
Arguments:
- slc: bfloat16 [2, 160, 16, 256], P(None, ('grp', 'date'), None, 'pix'), parts along dimension 1, may hold values from -3 to 3
- pairs: int32 [224, 2], P('grp'), parts along dimension 0, may hold values from 0 to 79, as said below
Outputs:
- phases: float32 [2, 160, 16, 256], P(None, ('grp', 'date'), None, 'pix'), parts along dimension 1
There are 2 independent parts, one for each index of `grp`. A program takes and returns all parts, laid end to end along the dimension named above; each array names one. Nothing has to cross between parts.
Inputs may be any that keep to these rules, and one draw needn't show every extreme that they name: `pairs`: each row is (i, j) with i < j <= i + 10; rows are distinct; at most 28 rows have i in one aligned block of 10 dates, and some block has exactly 28; some row has j = i + 10.
All inputs are finite; a program needn't handle non-finite values.
Results may differ from a plain program's by a relative error of at most 0.0003.
Values may be sent and summed in bfloat16 or wider, within the bound.
No kernel may reach another device: no remote copies, remote signals or barrier semaphores. Data moves between devices by JAX's collectives and lax.ppermute only.
A program may use at most 64 MiB of HBM per device.

v0:
```python
import functools

import jax
import jax.numpy as jnp
from jax import lax
from jax.experimental import pallas as pl
from jax.experimental.pallas import tpu as pltpu
from jax.sharding import PartitionSpec as P


WIN = 2
GAP = 10
LANES = 128


def pack_edges(slc_ref, near_ref, edge_ref):
    tiles, rows, cols = slc_ref.shape
    lead = (1 - lax.axis_index("pix")) * WIN
    lane = lax.broadcasted_iota(jnp.int32, (rows, cols), 1)
    acc = jnp.zeros((rows, cols), jnp.float32)
    for t in range(tiles):
        moved = pltpu.roll(slc_ref[t].astype(jnp.float32), lead + WIN * t, 1)
        acc = jnp.where((lane >= WIN * t) & (lane < WIN * (t + 1)), moved, acc)
    near_ref[...] = slc_ref[...]
    edge_ref[...] = acc.astype(edge_ref.dtype)


def place():
    block = lax.axis_index("date")
    return block % 2, (block // 2) % 2, block // 2


def select_kernel(pairs_ref, list_i, list_j, second, third, counts, band_ref, *, dates, unroll, local_cap):
    cols = band_ref.shape[1]
    odd, _, chip = place()
    base = dates * (2 * chip - 3)
    own = base + (3 + odd) * dates
    inner = base + 3 * dates
    row = lax.broadcasted_iota(jnp.int32, band_ref.shape, 0)
    column = lax.broadcasted_iota(jnp.int32, band_ref.shape, 1)
    apart = jnp.where(row < cols, row, row - 2 * cols * lax.axis_index("pix")) - column
    band_ref[...] = jnp.where((apart <= WIN) & (apart >= -WIN), 1.0, 0.0).astype(band_ref.dtype)

    def one(p, found):
        near, other, n2, n3 = found
        i, j = pairs_ref[2 * p], pairs_ref[2 * p + 1]

        def within(low, high):
            return ((j >= low) & (i < high)).astype(jnp.int32)

        local = ((i >= inner) & (j < inner + 2 * dates)).astype(jnp.int32)
        where = jnp.where(local == 1, near, other)
        list_i[where] = i - base
        list_j[where] = j - base
        second[n2] = where
        third[n3] = where
        return (
            near + local,
            other + (1 - local) * within(own - 2 * dates, own + 3 * dates),
            n2 + within(own - dates, own + 2 * dates),
            n3 + within(own, own + dates),
        )

    def four(q, found):
        for u in range(4):
            found = one(4 * q + u, found)
        return found

    zero = jnp.int32(0)
    total = pairs_ref.shape[0] // 2
    found = (zero, jnp.int32(local_cap), zero, zero)
    found = lax.fori_loop(0, total // 4, four, found)
    near, other, n2, n3 = lax.fori_loop(total // 4 * 4, total, one, found)
    for u in range(unroll):
        list_i[near + u] = 5 * dates
        list_j[near + u] = 5 * dates
        list_i[other + u] = 8 * dates
        list_j[other + u] = 8 * dates
        second[n2 + u] = other
        third[n3 + u] = other
    counts[0] = near
    counts[1] = other - local_cap
    counts[2] = n2
    counts[3] = n3


def make_boxes(rows, stage, band_ref):
    pitch = rows + 8

    def boxes(centers, halos):
        values = jnp.concatenate([jnp.concatenate(centers, axis=0), jnp.concatenate(halos, axis=0)], axis=1)
        high = values.astype(jnp.bfloat16)
        low = (values - high.astype(jnp.float32)).astype(jnp.bfloat16)
        band = band_ref[...]
        wide = jnp.dot(high, band, preferred_element_type=jnp.float32)
        wide = wide + jnp.dot(low, band, preferred_element_type=jnp.float32)
        results = []
        for slot in range(len(centers)):
            start = 8 + slot * pitch
            result = wide[slot * rows : (slot + 1) * rows]
            stage[pl.ds(start, rows), :] = result
            for shift in range(1, WIN + 1):
                result = result + stage[pl.ds(start - shift, rows), :]
                result = result + stage[pl.ds(start + shift, rows), :]
            results.append(result)
        return results

    return boxes


def loader(dates, cols, width, boxes, fields):
    sre, sim, hre, him, power = fields
    pix = lax.axis_index("pix")

    def load(ref, first, edge, target):
        edge = pltpu.roll(edge.astype(jnp.float32), -WIN * pix & (cols - 1), 1)
        for start in range(0, dates, width):
            squares, rims = [], []
            for k in range(start, start + width):
                re = ref[first + k].astype(jnp.float32)
                im = ref[first + dates + k].astype(jnp.float32)
                hr = pltpu.roll(edge, -WIN * k & (cols - 1), 1)
                hi = pltpu.roll(edge, -WIN * (dates + k) & (cols - 1), 1)
                sre[target + k] = re
                sim[target + k] = im
                hre[target + k] = hr
                him[target + k] = hi
                squares.append(re * re + im * im)
                rims.append(hr * hr + hi * hi)
            for u, value in enumerate(boxes(squares, rims)):
                power[target + start + u] = value

    return load


def coherer(boxes, fields, sums, offset, list_i, list_j, cre, cim, width):
    sre, sim, hre, him, power = fields
    are, aim = sums

    def cross(fr, fi, sr, si):
        return [fr * sr + fi * si, fi * sr - fr * si]

    def several(first):
        ends, centers, halos, scales = [], [], [], []
        for u in range(width):
            i, j = list_i[first + u] - offset, list_j[first + u] - offset
            ends.append((i, j))
            centers += cross(sre[i], sim[i], sre[j], sim[j])
            halos += cross(hre[i], him[i], hre[j], him[j])
            scales.append(2.0 / (power[i] + power[j]))
        sums_of = boxes(centers, halos)
        for u, (i, j) in enumerate(ends):
            re, im = sums_of[2 * u] * scales[u], sums_of[2 * u + 1] * scales[u]
            cre[first + u] = re
            cim[first + u] = im
            ri, rj, ii, ij = are[i], are[j], aim[i], aim[j]
            are[i] = ri + re
            are[j] = rj + re
            aim[i] = ii + im
            aim[j] = ij - im

    return several


def groups(first, count, width, body):
    def one(q, carry):
        body(first + q * width)
        return carry

    lax.fori_loop(0, (count + width - 1) // width, one, 0)


def near_kernel(
    list_i, list_j, counts, band_ref, mine_ref, mate_ref, edge_mine_ref, edge_mate_ref,
    sre, sim, hre, him, power, are, aim, cre, cim, stage, *, dates, unroll, width,
):
    _, rows, cols = sre.shape
    odd, _, _ = place()
    stage[...] = jnp.zeros_like(stage)
    boxes = make_boxes(rows, stage, band_ref)
    fields = (sre, sim, hre, him, power)
    load = loader(dates, cols, width, boxes, fields)
    load(mine_ref, 0, edge_mine_ref[...], odd * dates)
    load(mate_ref, 0, edge_mate_ref[...], (1 - odd) * dates)
    are[...] = jnp.ones_like(are)
    aim[...] = jnp.zeros_like(aim)
    groups(
        0, counts[0], unroll,
        coherer(boxes, fields, (are, aim), 3 * dates, list_i, list_j, cre, cim, unroll),
    )


def link_kernel(
    list_i, list_j, second, third, counts, band_ref, cross_ref, za_ref, zb_ref,
    nsre, nsim, nhre, nhim, npower, nare, naim, ncre, ncim, out_ref,
    sre, sim, hre, him, power, are, aim, bre, bim, cre, cim, stage, *, unroll, width, local_cap,
):
    _, dates, rows, cols = out_ref.shape
    tiles = 2 * dates + 1
    odd, far, _ = place()
    own = (3 + odd) * dates
    inner = 3 * dates
    stage[...] = jnp.zeros_like(stage)
    boxes = make_boxes(rows, stage, band_ref)
    fields = (sre, sim, hre, him, power)
    load = loader(dates, cols, width, boxes, fields)
    local, others, n2, n3 = counts[0], counts[1], counts[2], counts[3]

    sources = (nsre, nsim, nhre, nhim, npower, nare, naim)
    for source, target in zip(sources, (*fields, are, aim), strict=True):
        target[pl.ds(inner, 2 * dates)] = source[pl.ds(0, 2 * dates)]
    for low in (0, inner + 2 * dates):
        are[pl.ds(low, inner)] = jnp.ones((inner, rows, cols), jnp.float32)
        aim[pl.ds(low, inner)] = jnp.zeros((inner, rows, cols), jnp.float32)

    def keep(first):
        for u in range(unroll):
            cre[first + u] = ncre[first + u]
            cim[first + u] = ncim[first + u]

    groups(0, local, unroll, keep)

    load(cross_ref, 0, cross_ref[tiles - 1], 7 * odd * dates)
    up, down = 5 - 4 * far, 1 + 4 * far
    load(za_ref, 0, za_ref[tiles - 1], (up + odd) * dates)
    load(za_ref, tiles, za_ref[2 * tiles - 1], (up + 1 - odd) * dates)
    load(zb_ref, 0, zb_ref[tiles - 1], (down + odd) * dates)
    load(zb_ref, tiles, zb_ref[2 * tiles - 1], (down + 1 - odd) * dates)

    groups(
        local_cap, others, unroll,
        coherer(boxes, fields, (are, aim), 0, list_i, list_j, cre, cim, unroll),
    )

    def scaled(re, im):
        scale = lax.rsqrt(jnp.maximum(re * re + im * im, 1.0))
        return re * scale, im * scale

    def settle(low, count, xr, xi, yr, yi):
        def one(q, carry):
            for u in range(width):
                w = low + width * q + u
                re, im = scaled(xr[w], xi[w])
                xr[w] = re
                xi[w] = im
                yr[w] = re
                yi[w] = im
            return carry

        lax.fori_loop(0, count // width, one, 0)

    def step(index, count, xr, xi, yr, yi):
        def several(first):
            for u in range(unroll):
                p = index[first + u]
                i, j = list_i[p], list_j[p]
                re, im = cre[p], cim[p]
                nr, ni, fr, fi = xr[i], xi[i], xr[j], xi[j]
                ri, rj, ii, ij = yr[i], yr[j], yi[i], yi[j]
                yr[i] = ri + (re * fr - im * fi)
                yr[j] = rj + (re * nr + im * ni)
                yi[i] = ii + (re * fi + im * fr)
                yi[j] = ij + (re * ni - im * nr)

        groups(0, count, unroll, several)

    settle(own - 2 * dates, 5 * dates, are, aim, bre, bim)
    step(second, n2, are, aim, bre, bim)
    settle(own - dates, 3 * dates, bre, bim, are, aim)
    step(third, n3, bre, bim, are, aim)
    for k in range(dates):
        re, im = scaled(are[own + k], aim[own + k])
        out_ref[0, k] = re
        out_ref[1, k] = im


def swap(array, axis, matching):
    return lax.ppermute(array, axis, [*matching, *((j, i) for i, j in matching)])


def on_device(slc, pairs):
    comps, dates, rows, cols = slc.shape
    size = lax.axis_size("date")
    pair_count = pairs.shape[0]
    assert lax.axis_size("pix") == 2 and size % 2 == 0 and cols == LANES
    assert GAP <= dates and dates % 2 == 0 and comps * dates * WIN <= cols and rows % 8 == 0

    vmem = pl.BlockSpec(memory_space=pltpu.VMEM)
    smem = pl.BlockSpec(memory_space=pltpu.SMEM)

    def held(array):
        return pltpu.with_memory_space_constraint(array, pltpu.VMEM)

    def matching(step, keep):
        return [(i, i + step) for i in range(size - step) if keep(i)]

    main = slc.reshape(comps * dates, rows, cols)
    mates = matching(1, lambda i: i % 2 == 0)
    mate = swap(main, "date", mates)
    near, edge = pl.pallas_call(
        pack_edges,
        out_shape=[pltpu.VMEM(main.shape, slc.dtype), pltpu.VMEM((rows, cols), slc.dtype)],
        in_specs=[vmem],
        out_specs=[vmem] * 2,
    )(main)
    edge_mine = swap(edge, "pix", [(0, 1)])
    edge_mate = swap(edge, ("date", "pix"), [(2 * i + p, 2 * j + 1 - p) for i, j in mates for p in (0, 1)])
    cross = jnp.concatenate([near, edge_mine[None]], axis=0)
    both = jnp.concatenate([cross, mate, edge_mate[None]], axis=0)
    cross = swap(cross, "date", matching(3, lambda i: i % 2 == 1))
    za = swap(both, "date", matching(2, lambda i: i // 2 % 2 == 0))
    zb = swap(both, "date", matching(2, lambda i: i // 2 % 2 == 1))

    unroll = max(1, 128 // rows)
    width = max(w for w in range(1, 2 * unroll + 1) if dates % w == 0)
    per_block = min(pair_count, 2 * pair_count // size)
    local_cap = min(pair_count, 2 * per_block) + unroll
    cap = local_cap + min(pair_count, 6 * per_block) + unroll
    window = 8 * dates + 1
    stage = pltpu.VMEM((16 + max(width, 2 * unroll) * (rows + 8), cols), jnp.float32)
    plane = 4 * rows * cols
    spare = 4 * 1024 * 1024 + 64 * plane
    lists = pl.pallas_call(
        functools.partial(select_kernel, dates=dates, unroll=unroll, local_cap=local_cap),
        out_shape=[pltpu.SMEM((n,), jnp.int32) for n in (cap, cap, pair_count + unroll, pair_count + unroll, 4)]
        + [pltpu.VMEM((2 * cols, cols), jnp.bfloat16)],
        in_specs=[smem],
        out_specs=[smem] * 5 + [vmem],
    )(pairs.reshape(-1))
    band = held(lists[5])
    lists = [pltpu.with_memory_space_constraint(v, pltpu.SMEM) for v in lists[:5]]
    local = pl.pallas_call(
        functools.partial(near_kernel, dates=dates, unroll=unroll, width=width),
        out_shape=[pltpu.VMEM((2 * dates + 1, rows, cols), jnp.float32)] * 7
        + [pltpu.VMEM((local_cap, rows, cols), jnp.float32)] * 2,
        in_specs=[smem] * 3 + [vmem] * 5,
        out_specs=[vmem] * 9,
        scratch_shapes=[stage],
        compiler_params=pltpu.CompilerParams(vmem_limit_bytes=spare),
    )(lists[0], lists[1], lists[4], band, held(near), held(mate), held(edge_mine), held(edge_mate))
    field = pltpu.VMEM((window, rows, cols), jnp.float32)
    pair_field = pltpu.VMEM((cap, rows, cols), jnp.float32)
    return pl.pallas_call(
        functools.partial(link_kernel, unroll=unroll, width=width, local_cap=local_cap),
        out_shape=jax.ShapeDtypeStruct((comps, dates, rows, cols), jnp.float32),
        in_specs=[smem] * 5 + [vmem] * 13,
        out_specs=vmem,
        scratch_shapes=[field] * 9 + [pair_field] * 2 + [stage],
        compiler_params=pltpu.CompilerParams(vmem_limit_bytes=spare + (9 * window + 2 * cap) * plane),
    )(*lists, band, held(cross), held(za), held(zb), *(held(v) for v in local))


def solution(mesh):
    in_specs = (P(None, ("grp", "date"), None, "pix"), P("grp", None))
    out_specs = P(None, ("grp", "date"), None, "pix")

    return jax.shard_map(
        on_device, mesh=mesh, in_specs=in_specs, out_specs=out_specs, check_vma=False
    )
```

profile of v0, /device:TPU:5, one launch (start us, length us, event | category | flops | bytes accessed | tf_op | source)
XLA Modules:
  0.0 23.3 jit_solution(2074295980491904172)
XLA Ops:
  0.0 0.0 collective-permute-start.2
  0.0 1.0 %shard_map.29 = (bf16[20,16,128]{2,1,0:T(8,128)(2,1)S(1)}, bf16[16,128]{1,0:T(8,128)(2,1)S(1)}) custom-call(bf16[20,16,128]{2,1,0:T(8,128)(2,1)} %bitcast.7), custom_call_target="tpu_custom_call" | custom-call | tf_op jit(solution)/shard_map/pallas_call | solution.py:300
  1.0 2.4 %collective-permute-start.3 = (bf16[16,128]{1,0:T(8,128)(2,1)S(1)}, bf16[16,128]{1,0:T(8,128)(2,1)S(1)}, u32[]{:S(2)}, u32[]{:S(2)}) collective-permute-start(bf16[16,128]{1,0:T(8,128)(2,1)S(1)} %get-tuple-element.29), channel_id=1, source_target_pairs={{0,3},{1,2},{4,7},{5,6},{8,11},{9,10},{12,15},{13,14},{3,0},{2,1},... | collective-permute-start | bytes 12296 | tf_op jit(solution)/shard_map/ppermute | solution.py:278
  3.4 0.0 collective-permute-start
  3.4 1.6 %collective-permute-done.3.edge_mate_ref = bf16[16,128]{1,0:T(8,128)(2,1)S(1)} collective-permute-done((bf16[16,128]{1,0:T(8,128)(2,1)S(1)}, bf16[16,128]{1,0:T(8,128)(2,1)S(1)}, u32[]{:S(2)}, u32[]{:S(2)}) %collective-permute-start.3) | collective-permute-done | bytes 4128 | tf_op jit(solution)/shard_map/ppermute | solution.py:278
  5.0 0.0 collective-permute-done.edge_mine_ref
  5.0 0.0 collective-permute-done.2.mate_ref
  5.0 0.0 copy-start
  5.0 0.7 %collective-permute-start.5 = (bf16[42,16,128]{2,1,0:T(8,128)(2,1)S(1)}, bf16[42,16,128]{2,1,0:T(8,128)(2,1)S(1)}, u32[]{:S(2)}, u32[]{:S(2)}) collective-permute-start(bf16[42,16,128]{2,1,0:T(8,128)(2,1)S(1)} %pad_maximum_fusion), channel_id=1, source_target_pairs={{4,8},{6,10},{8,4},{10,6},{5,9},{7,11},{9,5},{11,7},{20,24},{22,26... | collective-permute-start | bytes 516104 | tf_op jit(solution)/shard_map/ppermute | solution.py:278
  5.7 3.9 %collective-permute-start.4 = (bf16[42,16,128]{2,1,0:T(8,128)(2,1)S(1)}, bf16[42,16,128]{2,1,0:T(8,128)(2,1)S(1)}, u32[]{:S(2)}, u32[]{:S(2)}) collective-permute-start(bf16[42,16,128]{2,1,0:T(8,128)(2,1)S(1)} %pad_maximum_fusion), channel_id=1, source_target_pairs={{0,4},{2,6},{8,12},{10,14},{4,0},{6,2},{12,8},{14,10},{1,5},{3,7},... | collective-permute-start | bytes 516104 | tf_op jit(solution)/shard_map/ppermute | solution.py:278
  9.6 2.1 %collective-permute-start.1 = (bf16[21,16,128]{2,1,0:T(8,128)(2,1)S(1)}, bf16[21,16,128]{2,1,0:T(8,128)(2,1)S(1)}, u32[]{:S(2)}, u32[]{:S(2)}) collective-permute-start(bf16[21,16,128]{2,1,0:T(8,128)(2,1)S(1)} %pad_maximum_fusion.1), channel_id=1, source_target_pairs={{2,8},{6,12},{8,2},{12,6},{3,9},{7,13},{9,3},{13,7},{18,24},{22,28... | collective-permute-start | bytes 258056 | tf_op jit(solution)/shard_map/ppermute | solution.py:278
  11.8 0.0 copy-done
  11.8 0.1 copy.3
  11.9 0.7 %reshape.6.pairs_ref = s32[224]{0:T(256)} reshape(s32[112,2]{1,0:T(8,128)S(1)} %copy.3) | data formatting | bytes 1792 | tf_op jit(solution)/shard_map/reshape | solution.py:329
  12.6 2.5 %shard_map.28 = (s32[184]{0:T(256)S(4)}, s32[184]{0:T(256)S(4)}, s32[120]{0:T(128)S(4)}, s32[120]{0:T(128)S(4)}, s32[4]{0:T(128)S(4)}, /*index=5*/bf16[256,128]{1,0:T(8,128)(2,1)S(1)}) custom-call(s32[224]{0:T(256)} %reshape.6.pairs_ref), custom_call_target="tpu_custom_call" | custom-call | tf_op jit(solution)/shard_map/pallas_call | solution.py:323
  15.1 1.4 %shard_map.30 = (f32[21,16,128]{2,1,0:T(8,128)S(1)}, f32[21,16,128]{2,1,0:T(8,128)S(1)}, f32[21,16,128]{2,1,0:T(8,128)S(1)}, f32[21,16,128]{2,1,0:T(8,128)S(1)},...) custom-call(s32[184]{0:T(256)S(4)} %get-tuple-element.22.list_i, ...), custom_call_target="tpu_custom_call" | custom-call | tf_op jit(solution)/shard_map/pallas_call | solution.py:332
  16.5 2.9 %collective-permute-done.1.cross_ref = bf16[21,16,128]{2,1,0:T(8,128)(2,1)S(1)} collective-permute-done((bf16[21,16,128]{2,1,0:T(8,128)(2,1)S(1)}, bf16[21,16,128]{2,1,0:T(8,128)(2,1)S(1)}, u32[]{:S(2)}, u32[]{:S(2)}) %collective-permute-start.1) | collective-permute-done | bytes 86048 | tf_op jit(solution)/shard_map/ppermute | solution.py:278
  19.4 0.0 collective-permute-done.5.zb_ref
  19.4 0.0 collective-permute-done.4.za_ref
  19.4 3.9 %shard_map.31 = f32[2,10,16,128]{3,2,1,0:T(8,128)} custom-call(s32[184]{0:T(256)S(4)} %get-tuple-element.22.list_i, s32[184]{0:T(256)S(4)} %get-tuple-element.23.list_j, s32[120]{0:T(128)S(4)} %get-tuple-element.24.second, s32[120]{0:T(128)S(4)} %get-tuple-element.25.third, s32[4]{0:T(128)S(4)} %get-tuple-element.26.counts, ...), custom_call_target="tpu_custom_call" | custom-call | tf_op jit(solution)/shard_map/pallas_call | solution.py:343
  (2 shorter events, 0.0 us)
Async XLA Ops:
  0.0 5.0 %collective-permute-start.2 = (bf16[20,16,128]{2,1,0:T(8,128)(2,1)}, bf16[20,16,128]{2,1,0:T(8,128)(2,1)S(1)}, u32[]{:S(2)}, u32[]{:S(2)}) collective-permute-start(bf16[20,16,128]{2,1,0:T(8,128)(2,1)} %bitcast.6), channel_id=1, source_target_pairs={{0,2},{4,6},{8,10},{12,14},{2,0},{6,4},{10,8},{14,12},{1,3},{5,7},... | collective-permute-start | bytes 245768 | tf_op jit(solution)/shard_map/ppermute | solution.py:278
  1.0 4.0 %collective-permute-start.3 = (bf16[16,128]{1,0:T(8,128)(2,1)S(1)}, bf16[16,128]{1,0:T(8,128)(2,1)S(1)}, u32[]{:S(2)}, u32[]{:S(2)}) collective-permute-start(bf16[16,128]{1,0:T(8,128)(2,1)S(1)} %get-tuple-element.29), channel_id=1, source_target_pairs={{0,3},{1,2},{4,7},{5,6},{8,11},{9,10},{12,15},{13,14},{3,0},{2,1},... | collective-permute-start | bytes 12296 | tf_op jit(solution)/shard_map/ppermute | solution.py:278
  3.4 1.6 %collective-permute-start = (bf16[16,128]{1,0:T(8,128)(2,1)S(1)}, bf16[16,128]{1,0:T(8,128)(2,1)S(1)}, u32[]{:S(2)}, u32[]{:S(2)}) collective-permute-start(bf16[16,128]{1,0:T(8,128)(2,1)S(1)} %get-tuple-element.29), channel_id=1, source_target_pairs={{0,1},{1,0},{2,3},{3,2},{4,5},{5,4},{6,7},{7,6},{8,9},{9,8},{10,11... | collective-permute-start | bytes 12296 | tf_op jit(solution)/shard_map/ppermute | solution.py:278
  5.0 6.7 %copy-start = (s32[112,2]{0,1:T(2,128)S(1)}, s32[112,2]{0,1:T(2,128)}, u32[]{:S(2)}) copy-start(s32[112,2]{0,1:T(2,128)} %param.3) | copy-start | bytes 2692
  5.0 14.4 %collective-permute-start.5 = (bf16[42,16,128]{2,1,0:T(8,128)(2,1)S(1)}, bf16[42,16,128]{2,1,0:T(8,128)(2,1)S(1)}, u32[]{:S(2)}, u32[]{:S(2)}) collective-permute-start(bf16[42,16,128]{2,1,0:T(8,128)(2,1)S(1)} %pad_maximum_fusion), channel_id=1, source_target_pairs={{4,8},{6,10},{8,4},{10,6},{5,9},{7,11},{9,5},{11,7},{20,24},{22,26... | collective-permute-start | bytes 516104 | tf_op jit(solution)/shard_map/ppermute | solution.py:278
  5.7 13.7 %collective-permute-start.4 = (bf16[42,16,128]{2,1,0:T(8,128)(2,1)S(1)}, bf16[42,16,128]{2,1,0:T(8,128)(2,1)S(1)}, u32[]{:S(2)}, u32[]{:S(2)}) collective-permute-start(bf16[42,16,128]{2,1,0:T(8,128)(2,1)S(1)} %pad_maximum_fusion), channel_id=1, source_target_pairs={{0,4},{2,6},{8,12},{10,14},{4,0},{6,2},{12,8},{14,10},{1,5},{3,7},... | collective-permute-start | bytes 516104 | tf_op jit(solution)/shard_map/ppermute | solution.py:278
  9.6 9.8 %collective-permute-start.1 = (bf16[21,16,128]{2,1,0:T(8,128)(2,1)S(1)}, bf16[21,16,128]{2,1,0:T(8,128)(2,1)S(1)}, u32[]{:S(2)}, u32[]{:S(2)}) collective-permute-start(bf16[21,16,128]{2,1,0:T(8,128)(2,1)S(1)} %pad_maximum_fusion.1), channel_id=1, source_target_pairs={{2,8},{6,12},{8,2},{12,6},{3,9},{7,13},{9,3},{13,7},{18,24},{22,28... | collective-permute-start | bytes 258056 | tf_op jit(solution)/shard_map/ppermute | solution.py:278
where the time goes:
time: 23.5 us; the launch traced here: 23.3 us
  starting transfers between devices  9.08 us (39%)
  Pallas kernels  8.76 us (37%)
  waiting for transfers between devices  4.53 us (19%)
  local copies, waits for them, and re-layouts  0.82 us (3%)
    ppermute x6, starting transfers between devices, swap(): lax.ppermute(array, axis, [*matching, *((j, i) for i, j in matching)])  9.08 us
    ppermute x6, waiting for transfers between devices, swap(): lax.ppermute(array, axis, [*matching, *((j, i) for i, j in matching)])  4.53 us
    pallas_call x1, Pallas kernels, on_device(): pl.pallas_call(functools.partial(link_kernel, unroll=unroll, width=width,...  3.86 us
    pallas_call x1, Pallas kernels, on_device(): pl.pallas_call(functools.partial(select_kernel, dates=dates, unroll=unrol...  2.47 us
    pallas_call x1, Pallas kernels, on_device(): pl.pallas_call(functools.partial(near_kernel, dates=dates, unroll=unroll,...  1.41 us
    pallas_call x1, Pallas kernels, on_device(): pl.pallas_call(pack_edges, out_shape=[pltpu.VMEM(main.shape, slc.dtype),...  1.01 us
    reshape x1, local copies, waits for them, and re-layouts, on_device(): pairs.reshape(-1)  0.7 us
  transfers between devices with their start and end apart: 6, of which 2 were waited for; matrix products, arithmetic and copies ran while one was open for 4% of the time, Pallas kernels for 21%

commit v1 on v0

--- a/solution.py
+++ b/solution.py
@@ -11,6 +11,7 @@
 WIN = 2
 GAP = 10
 LANES = 128
+SPARE = 3
 
 
 def pack_edges(slc_ref, near_ref, edge_ref):
@@ -43,7 +44,7 @@
 
     def one(p, found):
         near, other, n2, n3 = found
-        i, j = pairs_ref[2 * p], pairs_ref[2 * p + 1]
+        i, j = pairs_ref[0, p], pairs_ref[1, p]
 
         def within(low, high):
             return ((j >= low) & (i < high)).astype(jnp.int32)
@@ -67,15 +68,16 @@
         return found
 
     zero = jnp.int32(0)
-    total = pairs_ref.shape[0] // 2
+    total = pairs_ref.shape[1]
     found = (zero, jnp.int32(local_cap), zero, zero)
     found = lax.fori_loop(0, total // 4, four, found)
     near, other, n2, n3 = lax.fori_loop(total // 4 * 4, total, one, found)
-    for u in range(unroll):
-        list_i[near + u] = 5 * dates
-        list_j[near + u] = 5 * dates
+    for u in range(SPARE * unroll):
+        list_i[near + u] = 8 * dates
+        list_j[near + u] = 8 * dates
         list_i[other + u] = 8 * dates
         list_j[other + u] = 8 * dates
+    for u in range(unroll):
         second[n2 + u] = other
         third[n3 + u] = other
     counts[0] = near
@@ -87,29 +89,30 @@
 def make_boxes(rows, stage, band_ref):
     pitch = rows + 8
 
-    def boxes(centers, halos):
+    def spread(centers, halos, slot):
         values = jnp.concatenate([jnp.concatenate(centers, axis=0), jnp.concatenate(halos, axis=0)], axis=1)
         high = values.astype(jnp.bfloat16)
         low = (values - high.astype(jnp.float32)).astype(jnp.bfloat16)
         band = band_ref[...]
         wide = jnp.dot(high, band, preferred_element_type=jnp.float32)
         wide = wide + jnp.dot(low, band, preferred_element_type=jnp.float32)
-        results = []
-        for slot in range(len(centers)):
-            start = 8 + slot * pitch
-            result = wide[slot * rows : (slot + 1) * rows]
-            stage[pl.ds(start, rows), :] = result
-            for shift in range(1, WIN + 1):
-                result = result + stage[pl.ds(start - shift, rows), :]
-                result = result + stage[pl.ds(start + shift, rows), :]
-            results.append(result)
-        return results
-
-    return boxes
+        for k in range(len(centers)):
+            stage[pl.ds(8 + (slot + k) * pitch, rows), :] = wide[k * rows : (k + 1) * rows]
+
+    def gather(slot):
+        start = 8 + slot * pitch
+        result = stage[pl.ds(start, rows), :]
+        for shift in range(1, WIN + 1):
+            result = result + stage[pl.ds(start - shift, rows), :]
+            result = result + stage[pl.ds(start + shift, rows), :]
+        return result
+
+    return spread, gather
 
 
 def loader(dates, cols, width, boxes, fields):
     sre, sim, hre, him, power = fields
+    spread, gather = boxes
     pix = lax.axis_index("pix")
 
     def load(ref, first, edge, target):
@@ -127,39 +130,54 @@
                 him[target + k] = hi
                 squares.append(re * re + im * im)
                 rims.append(hr * hr + hi * hi)
-            for u, value in enumerate(boxes(squares, rims)):
-                power[target + start + u] = value
+            spread(squares, rims, 0)
+            for u in range(width):
+                power[target + start + u] = gather(u)
 
     return load
 
 
-def coherer(boxes, fields, sums, offset, list_i, list_j, cre, cim, width):
+def cohere(boxes, fields, sums, list_i, list_j, cre, cim, first, count, width):
     sre, sim, hre, him, power = fields
     are, aim = sums
+    spread, gather = boxes
 
     def cross(fr, fi, sr, si):
         return [fr * sr + fi * si, fi * sr - fr * si]
 
-    def several(first):
-        ends, centers, halos, scales = [], [], [], []
+    def multiply(group, half):
+        centers, halos = [], []
         for u in range(width):
-            i, j = list_i[first + u] - offset, list_j[first + u] - offset
-            ends.append((i, j))
+            p = first + group * width + u
+            i, j = list_i[p], list_j[p]
             centers += cross(sre[i], sim[i], sre[j], sim[j])
             halos += cross(hre[i], him[i], hre[j], him[j])
-            scales.append(2.0 / (power[i] + power[j]))
-        sums_of = boxes(centers, halos)
-        for u, (i, j) in enumerate(ends):
-            re, im = sums_of[2 * u] * scales[u], sums_of[2 * u + 1] * scales[u]
-            cre[first + u] = re
-            cim[first + u] = im
+        spread(centers, halos, 2 * width * half)
+
+    def finish(group, half):
+        for u in range(width):
+            p = first + group * width + u
+            i, j = list_i[p], list_j[p]
+            scale = 2.0 / (power[i] + power[j])
+            slot = 2 * (width * half + u)
+            re, im = gather(slot) * scale, gather(slot + 1) * scale
+            cre[p] = re
+            cim[p] = im
             ri, rj, ii, ij = are[i], are[j], aim[i], aim[j]
             are[i] = ri + re
             are[j] = rj + re
             aim[i] = ii + im
             aim[j] = ij - im
 
-    return several
+    def two(q, carry):
+        multiply(2 * q + 1, 1)
+        finish(2 * q, 0)
+        multiply(2 * q + 2, 0)
+        finish(2 * q + 1, 1)
+        return carry
+
+    multiply(0, 0)
+    lax.fori_loop(0, (count + 2 * width - 1) // (2 * width), two, 0)
 
 
 def groups(first, count, width, body):
@@ -172,7 +190,7 @@
 
 def near_kernel(
     list_i, list_j, counts, band_ref, mine_ref, mate_ref, edge_mine_ref, edge_mate_ref,
-    sre, sim, hre, him, power, are, aim, cre, cim, stage, *, dates, unroll, width,
+    sre, sim, hre, him, power, are, aim, cre, cim, stage, *, dates, batch, width,
 ):
     _, rows, cols = sre.shape
     odd, _, _ = place()
@@ -180,45 +198,27 @@
     boxes = make_boxes(rows, stage, band_ref)
     fields = (sre, sim, hre, him, power)
     load = loader(dates, cols, width, boxes, fields)
-    load(mine_ref, 0, edge_mine_ref[...], odd * dates)
-    load(mate_ref, 0, edge_mate_ref[...], (1 - odd) * dates)
+    load(mine_ref, 0, edge_mine_ref[...], (3 + odd) * dates)
+    load(mate_ref, 0, edge_mate_ref[...], (4 - odd) * dates)
     are[...] = jnp.ones_like(are)
     aim[...] = jnp.zeros_like(aim)
-    groups(
-        0, counts[0], unroll,
-        coherer(boxes, fields, (are, aim), 3 * dates, list_i, list_j, cre, cim, unroll),
-    )
+    cohere(boxes, fields, (are, aim), list_i, list_j, cre, cim, 0, counts[0], batch)
 
 
 def link_kernel(
-    list_i, list_j, second, third, counts, band_ref, cross_ref, za_ref, zb_ref,
-    nsre, nsim, nhre, nhim, npower, nare, naim, ncre, ncim, out_ref,
-    sre, sim, hre, him, power, are, aim, bre, bim, cre, cim, stage, *, unroll, width, local_cap,
+    list_i, list_j, second, third, counts, band_ref, cross_ref, za_ref, zb_ref, *refs,
+    batch, unroll, width, local_cap,
 ):
+    out_ref, sre, sim, hre, him, power, are, aim, cre, cim, bre, bim, stage = refs[9:]
     _, dates, rows, cols = out_ref.shape
     tiles = 2 * dates + 1
     odd, far, _ = place()
     own = (3 + odd) * dates
-    inner = 3 * dates
     stage[...] = jnp.zeros_like(stage)
     boxes = make_boxes(rows, stage, band_ref)
     fields = (sre, sim, hre, him, power)
     load = loader(dates, cols, width, boxes, fields)
-    local, others, n2, n3 = counts[0], counts[1], counts[2], counts[3]
-
-    sources = (nsre, nsim, nhre, nhim, npower, nare, naim)
-    for source, target in zip(sources, (*fields, are, aim), strict=True):
-        target[pl.ds(inner, 2 * dates)] = source[pl.ds(0, 2 * dates)]
-    for low in (0, inner + 2 * dates):
-        are[pl.ds(low, inner)] = jnp.ones((inner, rows, cols), jnp.float32)
-        aim[pl.ds(low, inner)] = jnp.zeros((inner, rows, cols), jnp.float32)
-
-    def keep(first):
-        for u in range(unroll):
-            cre[first + u] = ncre[first + u]
-            cim[first + u] = ncim[first + u]
-
-    groups(0, local, unroll, keep)
+    others, n2, n3 = counts[1], counts[2], counts[3]
 
     load(cross_ref, 0, cross_ref[tiles - 1], 7 * odd * dates)
     up, down = 5 - 4 * far, 1 + 4 * far
@@ -226,11 +226,7 @@
     load(za_ref, tiles, za_ref[2 * tiles - 1], (up + 1 - odd) * dates)
     load(zb_ref, 0, zb_ref[tiles - 1], (down + odd) * dates)
     load(zb_ref, tiles, zb_ref[2 * tiles - 1], (down + 1 - odd) * dates)
-
-    groups(
-        local_cap, others, unroll,
-        coherer(boxes, fields, (are, aim), 0, list_i, list_j, cre, cim, unroll),
-    )
+    cohere(boxes, fields, (are, aim), list_i, list_j, cre, cim, local_cap, others, batch)
 
     def scaled(re, im):
         scale = lax.rsqrt(jnp.maximum(re * re + im * im, 1.0))
@@ -312,12 +308,13 @@
     zb = swap(both, "date", matching(2, lambda i: i // 2 % 2 == 1))
 
     unroll = max(1, 128 // rows)
+    batch = max(1, 128 // rows)
     width = max(w for w in range(1, 2 * unroll + 1) if dates % w == 0)
     per_block = min(pair_count, 2 * pair_count // size)
-    local_cap = min(pair_count, 2 * per_block) + unroll
-    cap = local_cap + min(pair_count, 6 * per_block) + unroll
+    local_cap = min(pair_count, 2 * per_block) + SPARE * unroll
+    cap = local_cap + min(pair_count, 6 * per_block) + SPARE * unroll
     window = 8 * dates + 1
-    stage = pltpu.VMEM((16 + max(width, 2 * unroll) * (rows + 8), cols), jnp.float32)
+    stage = pltpu.VMEM((16 + max(width, 4 * batch) * (rows + 8), cols), jnp.float32)
     plane = 4 * rows * cols
     spare = 4 * 1024 * 1024 + 64 * plane
     lists = pl.pallas_call(
@@ -326,28 +323,28 @@
         + [pltpu.VMEM((2 * cols, cols), jnp.bfloat16)],
         in_specs=[smem],
         out_specs=[smem] * 5 + [vmem],
-    )(pairs.reshape(-1))
+    )(pairs.T)
     band = held(lists[5])
     lists = [pltpu.with_memory_space_constraint(v, pltpu.SMEM) for v in lists[:5]]
+    fields = [pltpu.VMEM((window, rows, cols), jnp.float32)] * 7 + [pltpu.VMEM((cap, rows, cols), jnp.float32)] * 2
     local = pl.pallas_call(
-        functools.partial(near_kernel, dates=dates, unroll=unroll, width=width),
-        out_shape=[pltpu.VMEM((2 * dates + 1, rows, cols), jnp.float32)] * 7
-        + [pltpu.VMEM((local_cap, rows, cols), jnp.float32)] * 2,
+        functools.partial(near_kernel, dates=dates, batch=batch, width=width),
+        out_shape=fields,
         in_specs=[smem] * 3 + [vmem] * 5,
         out_specs=[vmem] * 9,
         scratch_shapes=[stage],
         compiler_params=pltpu.CompilerParams(vmem_limit_bytes=spare),
     )(lists[0], lists[1], lists[4], band, held(near), held(mate), held(edge_mine), held(edge_mate))
-    field = pltpu.VMEM((window, rows, cols), jnp.float32)
-    pair_field = pltpu.VMEM((cap, rows, cols), jnp.float32)
-    return pl.pallas_call(
-        functools.partial(link_kernel, unroll=unroll, width=width, local_cap=local_cap),
-        out_shape=jax.ShapeDtypeStruct((comps, dates, rows, cols), jnp.float32),
+    linked = pl.pallas_call(
+        functools.partial(link_kernel, batch=batch, unroll=unroll, width=width, local_cap=local_cap),
+        out_shape=[jax.ShapeDtypeStruct((comps, dates, rows, cols), jnp.float32), *fields],
         in_specs=[smem] * 5 + [vmem] * 13,
-        out_specs=vmem,
-        scratch_shapes=[field] * 9 + [pair_field] * 2 + [stage],
-        compiler_params=pltpu.CompilerParams(vmem_limit_bytes=spare + (9 * window + 2 * cap) * plane),
+        out_specs=[vmem] * 10,
+        input_output_aliases={9 + k: 1 + k for k in range(9)},
+        scratch_shapes=[fields[0]] * 2 + [stage],
+        compiler_params=pltpu.CompilerParams(vmem_limit_bytes=spare + 2 * window * plane),
     )(*lists, band, held(cross), held(za), held(zb), *(held(v) for v in local))
+    return linked[0]
 
 
 def solution(mesh):

time: 23.5 us -> 23.3 us (level)
  local copies, waits for them, and re-layouts: 0.82 us -> 0 us
  waiting for transfers between devices: 4.53 us -> 5.24 us
    ppermute x6, waiting for transfers between devices: 4.53 us -> 5.24 us  [swap(): lax.ppermute(array, axis, [*matching, *((j, i) for i, j in matching)])]
    reshape x1 -> x0, local copies, waits for them, and re-layouts: 0.7 us -> none  [on_device(): pairs.reshape(-1)]
  transfers between devices with their start and end apart: 6 -> 6, of which waited for: 2 -> 2; matrix products, arithmetic and copies ran while one was open for 4% -> 0% of each run, Pallas kernels for 21% -> 22%
where the time goes in v1:
time: 23.3 us; the launch traced here: 23.1 us
  starting transfers between devices  9.08 us (39%)
  Pallas kernels  8.7 us (37%)
  waiting for transfers between devices  5.24 us (22%)
    ppermute x6, starting transfers between devices, swap(): lax.ppermute(array, axis, [*matching, *((j, i) for i, j in matching)])  9.08 us
    ppermute x6, waiting for transfers between devices, swap(): lax.ppermute(array, axis, [*matching, *((j, i) for i, j in matching)])  5.24 us
    pallas_call x1, Pallas kernels, on_device(): pl.pallas_call(functools.partial(link_kernel, batch=batch, unroll=unroll,...  3.69 us
    pallas_call x1, Pallas kernels, on_device(): pl.pallas_call(functools.partial(select_kernel, dates=dates, unroll=unrol...  2.62 us
    pallas_call x1, Pallas kernels, on_device(): pl.pallas_call(functools.partial(near_kernel, dates=dates, batch=batch, w...  1.39 us
    pallas_call x1, Pallas kernels, on_device(): pl.pallas_call(pack_edges, out_shape=[pltpu.VMEM(main.shape, slc.dtype),...  1.01 us
  transfers between devices with their start and end apart: 6, of which 2 were waited for; matrix products, arithmetic and copies ran while one was open for 0% of the time, Pallas kernels for 22%

profile of v1, /device:TPU:5, one launch (start us, length us, event | category | flops | bytes accessed | tf_op | source)
XLA Modules:
  0.0 23.1 jit_solution(13615200464335032623)
XLA Ops:
  0.0 0.0 collective-permute-start.2
  0.0 1.0 %shard_map.29 = (bf16[20,16,128]{2,1,0:T(8,128)(2,1)S(1)}, bf16[16,128]{1,0:T(8,128)(2,1)S(1)}) custom-call(bf16[20,16,128]{2,1,0:T(8,128)(2,1)} %bitcast.8), custom_call_target="tpu_custom_call" | custom-call | tf_op jit(solution)/shard_map/pallas_call | solution.py:296
  1.0 2.4 %collective-permute-start.3 = (bf16[16,128]{1,0:T(8,128)(2,1)S(1)}, bf16[16,128]{1,0:T(8,128)(2,1)S(1)}, u32[]{:S(2)}, u32[]{:S(2)}) collective-permute-start(bf16[16,128]{1,0:T(8,128)(2,1)S(1)} %get-tuple-element.30), channel_id=1, source_target_pairs={{0,3},{1,2},{4,7},{5,6},{8,11},{9,10},{12,15},{13,14},{3,0},{2,1},... | collective-permute-start | bytes 12296 | tf_op jit(solution)/shard_map/ppermute | solution.py:274
  3.4 0.0 collective-permute-start
  3.4 1.6 %collective-permute-done.3.edge_mate_ref = bf16[16,128]{1,0:T(8,128)(2,1)S(1)} collective-permute-done((bf16[16,128]{1,0:T(8,128)(2,1)S(1)}, bf16[16,128]{1,0:T(8,128)(2,1)S(1)}, u32[]{:S(2)}, u32[]{:S(2)}) %collective-permute-start.3) | collective-permute-done | bytes 4128 | tf_op jit(solution)/shard_map/ppermute | solution.py:274
  5.0 0.0 collective-permute-done.edge_mine_ref
  5.0 0.0 collective-permute-done.2.mate_ref
  5.0 0.7 %collective-permute-start.5 = (bf16[42,16,128]{2,1,0:T(8,128)(2,1)S(1)}, bf16[42,16,128]{2,1,0:T(8,128)(2,1)S(1)}, u32[]{:S(2)}, u32[]{:S(2)}) collective-permute-start(bf16[42,16,128]{2,1,0:T(8,128)(2,1)S(1)} %pad_maximum_fusion), channel_id=1, source_target_pairs={{4,8},{6,10},{8,4},{10,6},{5,9},{7,11},{9,5},{11,7},{20,24},{22,26... | collective-permute-start | bytes 516104 | tf_op jit(solution)/shard_map/ppermute | solution.py:274
  5.7 3.9 %collective-permute-start.4 = (bf16[42,16,128]{2,1,0:T(8,128)(2,1)S(1)}, bf16[42,16,128]{2,1,0:T(8,128)(2,1)S(1)}, u32[]{:S(2)}, u32[]{:S(2)}) collective-permute-start(bf16[42,16,128]{2,1,0:T(8,128)(2,1)S(1)} %pad_maximum_fusion), channel_id=1, source_target_pairs={{0,4},{2,6},{8,12},{10,14},{4,0},{6,2},{12,8},{14,10},{1,5},{3,7},... | collective-permute-start | bytes 516104 | tf_op jit(solution)/shard_map/ppermute | solution.py:274
  9.6 2.1 %collective-permute-start.1 = (bf16[21,16,128]{2,1,0:T(8,128)(2,1)S(1)}, bf16[21,16,128]{2,1,0:T(8,128)(2,1)S(1)}, u32[]{:S(2)}, u32[]{:S(2)}) collective-permute-start(bf16[21,16,128]{2,1,0:T(8,128)(2,1)S(1)} %pad_maximum_fusion.1), channel_id=1, source_target_pairs={{2,8},{6,12},{8,2},{12,6},{3,9},{7,13},{9,3},{13,7},{18,24},{22,28... | collective-permute-start | bytes 258056 | tf_op jit(solution)/shard_map/ppermute | solution.py:274
  11.7 2.6 %shard_map.28 = (s32[216]{0:T(256)S(4)}, s32[216]{0:T(256)S(4)}, s32[120]{0:T(128)S(4)}, s32[120]{0:T(128)S(4)}, s32[4]{0:T(128)S(4)}, /*index=5*/bf16[256,128]{1,0:T(8,128)(2,1)S(1)}) custom-call(s32[2,112]{1,0:T(2,128)} %bitcast.9), custom_call_target="tpu_custom_call" | custom-call | tf_op jit(solution)/shard_map/pallas_call | solution.py:320
  14.4 1.4 %shard_map.30 = (f32[81,16,128]{2,1,0:T(8,128)S(1)}, f32[81,16,128]{2,1,0:T(8,128)S(1)}, f32[81,16,128]{2,1,0:T(8,128)S(1)}, f32[81,16,128]{2,1,0:T(8,128)S(1)},...) custom-call(s32[216]{0:T(256)S(4)} %get-tuple-element.23.list_i, ...), custom_call_target="tpu_custom_call" | custom-call | tf_op jit(solution)/shard_map/pallas_call | solution.py:330
  15.8 3.6 %collective-permute-done.1.cross_ref = bf16[21,16,128]{2,1,0:T(8,128)(2,1)S(1)} collective-permute-done((bf16[21,16,128]{2,1,0:T(8,128)(2,1)S(1)}, bf16[21,16,128]{2,1,0:T(8,128)(2,1)S(1)}, u32[]{:S(2)}, u32[]{:S(2)}) %collective-permute-start.1) | collective-permute-done | bytes 86048 | tf_op jit(solution)/shard_map/ppermute | solution.py:274
  19.4 0.0 collective-permute-done.5.zb_ref
  19.4 0.0 collective-permute-done.4.za_ref
  19.4 3.7 %shard_map.31 = (f32[2,10,16,128]{3,2,1,0:T(8,128)}, f32[81,16,128]{2,1,0:T(8,128)S(1)}, f32[81,16,128]{2,1,0:T(8,128)S(1)}, f32[81,16,128]{2,1,0:T(8,128)S(1)},...) custom-call(s32[216]{0:T(256)S(4)} %get-tuple-element.23.list_i, ...), custom_call_target="tpu_custom_call", output_to_operand_aliasing={{1}: (9, {}), {2}: (10, {}), {3}: (11, {}), {4}: (12, {}), ... | custom-call | tf_op jit(solution)/shard_map/pallas_call | solution.py:338
  (2 shorter events, 0.0 us)
Async XLA Ops:
  0.0 5.0 %collective-permute-start.2 = (bf16[20,16,128]{2,1,0:T(8,128)(2,1)}, bf16[20,16,128]{2,1,0:T(8,128)(2,1)S(1)}, u32[]{:S(2)}, u32[]{:S(2)}) collective-permute-start(bf16[20,16,128]{2,1,0:T(8,128)(2,1)} %bitcast.7), channel_id=1, source_target_pairs={{0,2},{4,6},{8,10},{12,14},{2,0},{6,4},{10,8},{14,12},{1,3},{5,7},... | collective-permute-start | bytes 245768 | tf_op jit(solution)/shard_map/ppermute | solution.py:274
  1.0 4.0 %collective-permute-start.3 = (bf16[16,128]{1,0:T(8,128)(2,1)S(1)}, bf16[16,128]{1,0:T(8,128)(2,1)S(1)}, u32[]{:S(2)}, u32[]{:S(2)}) collective-permute-start(bf16[16,128]{1,0:T(8,128)(2,1)S(1)} %get-tuple-element.30), channel_id=1, source_target_pairs={{0,3},{1,2},{4,7},{5,6},{8,11},{9,10},{12,15},{13,14},{3,0},{2,1},... | collective-permute-start | bytes 12296 | tf_op jit(solution)/shard_map/ppermute | solution.py:274
  3.4 1.6 %collective-permute-start = (bf16[16,128]{1,0:T(8,128)(2,1)S(1)}, bf16[16,128]{1,0:T(8,128)(2,1)S(1)}, u32[]{:S(2)}, u32[]{:S(2)}) collective-permute-start(bf16[16,128]{1,0:T(8,128)(2,1)S(1)} %get-tuple-element.30), channel_id=1, source_target_pairs={{0,1},{1,0},{2,3},{3,2},{4,5},{5,4},{6,7},{7,6},{8,9},{9,8},{10,11... | collective-permute-start | bytes 12296 | tf_op jit(solution)/shard_map/ppermute | solution.py:274
  5.0 14.4 %collective-permute-start.5 = (bf16[42,16,128]{2,1,0:T(8,128)(2,1)S(1)}, bf16[42,16,128]{2,1,0:T(8,128)(2,1)S(1)}, u32[]{:S(2)}, u32[]{:S(2)}) collective-permute-start(bf16[42,16,128]{2,1,0:T(8,128)(2,1)S(1)} %pad_maximum_fusion), channel_id=1, source_target_pairs={{4,8},{6,10},{8,4},{10,6},{5,9},{7,11},{9,5},{11,7},{20,24},{22,26... | collective-permute-start | bytes 516104 | tf_op jit(solution)/shard_map/ppermute | solution.py:274
  5.7 13.7 %collective-permute-start.4 = (bf16[42,16,128]{2,1,0:T(8,128)(2,1)S(1)}, bf16[42,16,128]{2,1,0:T(8,128)(2,1)S(1)}, u32[]{:S(2)}, u32[]{:S(2)}) collective-permute-start(bf16[42,16,128]{2,1,0:T(8,128)(2,1)S(1)} %pad_maximum_fusion), channel_id=1, source_target_pairs={{0,4},{2,6},{8,12},{10,14},{4,0},{6,2},{12,8},{14,10},{1,5},{3,7},... | collective-permute-start | bytes 516104 | tf_op jit(solution)/shard_map/ppermute | solution.py:274
  9.6 9.8 %collective-permute-start.1 = (bf16[21,16,128]{2,1,0:T(8,128)(2,1)S(1)}, bf16[21,16,128]{2,1,0:T(8,128)(2,1)S(1)}, u32[]{:S(2)}, u32[]{:S(2)}) collective-permute-start(bf16[21,16,128]{2,1,0:T(8,128)(2,1)S(1)} %pad_maximum_fusion.1), channel_id=1, source_target_pairs={{2,8},{6,12},{8,2},{12,6},{3,9},{7,13},{9,3},{13,7},{18,24},{22,28... | collective-permute-start | bytes 258056 | tf_op jit(solution)/shard_map/ppermute | solution.py:274

commit v2 on v1

--- a/solution.py
+++ b/solution.py
@@ -271,7 +271,10 @@
 
 
 def swap(array, axis, matching):
-    return lax.ppermute(array, axis, [*matching, *((j, i) for i, j in matching)])
+    matched = {i for pair in matching for i in pair}
+    alone = [i for i in range(lax.axis_size(axis)) if i not in matched]
+    pairing = [*matching, *zip(alone[::2], alone[1::2], strict=True)]
+    return lax.ppermute(array, axis, [*pairing, *((j, i) for i, j in pairing)])
 
 
 def on_device(slc, pairs):

time: 23.3 us -> 21.1 us (0.906)
  the two profiles are of different devices: /device:TPU:5 before, /device:TPU:0 now
where the time goes in v2:
time: 21.1 us; the launch traced here: 21 us
  Pallas kernels  8.1 us (38%)
  starting transfers between devices  6.46 us (31%)
  waiting for transfers between devices  6.32 us (30%)
    ppermute x6, starting transfers between devices, swap(): return lax.ppermute(array, axis, [*pairing, *((j, i) for i, j in pairing)])  6.46 us
    ppermute x6, waiting for transfers between devices, swap(): return lax.ppermute(array, axis, [*pairing, *((j, i) for i, j in pairing)])  6.32 us
    pallas_call x1, Pallas kernels, on_device(): pl.pallas_call(functools.partial(link_kernel, batch=batch, unroll=unroll,...  3.09 us
    pallas_call x1, Pallas kernels, on_device(): pl.pallas_call(functools.partial(select_kernel, dates=dates, unroll=unrol...  2.62 us
    pallas_call x1, Pallas kernels, on_device(): pl.pallas_call(functools.partial(near_kernel, dates=dates, batch=batch, w...  1.38 us
    pallas_call x1, Pallas kernels, on_device(): pl.pallas_call(pack_edges, out_shape=[pltpu.VMEM(main.shape, slc.dtype),...  1.01 us
  transfers between devices with their start and end apart: 6, of which 2 were waited for; matrix products, arithmetic and copies ran while one was open for 0% of the time, Pallas kernels for 24%

profile of v2, /device:TPU:0, one launch (start us, length us, event | category | flops | bytes accessed | tf_op | source)
XLA Modules:
  0.0 21.0 jit_solution(4544467046534987700)
XLA Ops:
  0.0 3.0 %collective-permute-start.2 = (bf16[20,16,128]{2,1,0:T(8,128)(2,1)}, bf16[20,16,128]{2,1,0:T(8,128)(2,1)S(1)}, u32[]{:S(2)}, u32[]{:S(2)}) collective-permute-start(bf16[20,16,128]{2,1,0:T(8,128)(2,1)} %bitcast.7), channel_id=1, source_target_pairs={{0,2},{4,6},{8,10},{12,14},{2,0},{6,4},{10,8},{14,12},{1,3},{5,7},... | collective-permute-start | bytes 245768 | tf_op jit(solution)/shard_map/ppermute | solution.py:277
  3.0 1.0 %shard_map.29 = (bf16[20,16,128]{2,1,0:T(8,128)(2,1)S(1)}, bf16[16,128]{1,0:T(8,128)(2,1)S(1)}) custom-call(bf16[20,16,128]{2,1,0:T(8,128)(2,1)} %bitcast.8), custom_call_target="tpu_custom_call" | custom-call | tf_op jit(solution)/shard_map/pallas_call | solution.py:299
  4.0 0.1 collective-permute-start.3
  4.1 0.1 collective-permute-start
  4.2 2.9 %collective-permute-done.3.edge_mate_ref = bf16[16,128]{1,0:T(8,128)(2,1)S(1)} collective-permute-done((bf16[16,128]{1,0:T(8,128)(2,1)S(1)}, bf16[16,128]{1,0:T(8,128)(2,1)S(1)}, u32[]{:S(2)}, u32[]{:S(2)}) %collective-permute-start.3) | collective-permute-done | bytes 4128 | tf_op jit(solution)/shard_map/ppermute | solution.py:277
  7.1 0.0 collective-permute-done.edge_mine_ref
  7.1 0.0 collective-permute-done.2.mate_ref
  7.2 0.6 %collective-permute-start.5 = (bf16[42,16,128]{2,1,0:T(8,128)(2,1)S(1)}, bf16[42,16,128]{2,1,0:T(8,128)(2,1)S(1)}, u32[]{:S(2)}, u32[]{:S(2)}) collective-permute-start(bf16[42,16,128]{2,1,0:T(8,128)(2,1)S(1)} %pad_maximum_fusion), channel_id=1, source_target_pairs={{4,8},{6,10},{0,2},{12,14},{8,4},{10,6},{2,0},{14,12},{5,9},{7,11}... | collective-permute-start | bytes 516104 | tf_op jit(solution)/shard_map/ppermute | solution.py:277
  7.8 2.6 %collective-permute-start.4 = (bf16[42,16,128]{2,1,0:T(8,128)(2,1)S(1)}, bf16[42,16,128]{2,1,0:T(8,128)(2,1)S(1)}, u32[]{:S(2)}, u32[]{:S(2)}) collective-permute-start(bf16[42,16,128]{2,1,0:T(8,128)(2,1)S(1)} %pad_maximum_fusion), channel_id=1, source_target_pairs={{0,4},{2,6},{8,12},{10,14},{4,0},{6,2},{12,8},{14,10},{1,5},{3,7},... | collective-permute-start | bytes 516104 | tf_op jit(solution)/shard_map/ppermute | solution.py:277
  10.4 0.1 collective-permute-start.1
  10.5 2.6 %shard_map.28 = (s32[216]{0:T(256)S(4)}, s32[216]{0:T(256)S(4)}, s32[120]{0:T(128)S(4)}, s32[120]{0:T(128)S(4)}, s32[4]{0:T(128)S(4)}, /*index=5*/bf16[256,128]{1,0:T(8,128)(2,1)S(1)}) custom-call(s32[2,112]{1,0:T(2,128)} %bitcast.9), custom_call_target="tpu_custom_call" | custom-call | tf_op jit(solution)/shard_map/pallas_call | solution.py:323
  13.1 1.4 %shard_map.30 = (f32[81,16,128]{2,1,0:T(8,128)S(1)}, f32[81,16,128]{2,1,0:T(8,128)S(1)}, f32[81,16,128]{2,1,0:T(8,128)S(1)}, f32[81,16,128]{2,1,0:T(8,128)S(1)},...) custom-call(s32[216]{0:T(256)S(4)} %get-tuple-element.23.list_i, ...), custom_call_target="tpu_custom_call" | custom-call | tf_op jit(solution)/shard_map/pallas_call | solution.py:333
  14.5 3.4 %collective-permute-done.1.cross_ref = bf16[21,16,128]{2,1,0:T(8,128)(2,1)S(1)} collective-permute-done((bf16[21,16,128]{2,1,0:T(8,128)(2,1)S(1)}, bf16[21,16,128]{2,1,0:T(8,128)(2,1)S(1)}, u32[]{:S(2)}, u32[]{:S(2)}) %collective-permute-start.1) | collective-permute-done | bytes 86048 | tf_op jit(solution)/shard_map/ppermute | solution.py:277
  17.9 0.0 collective-permute-done.5.zb_ref
  17.9 0.0 collective-permute-done.4.za_ref
  17.9 3.1 %shard_map.31 = (f32[2,10,16,128]{3,2,1,0:T(8,128)}, f32[81,16,128]{2,1,0:T(8,128)S(1)}, f32[81,16,128]{2,1,0:T(8,128)S(1)}, f32[81,16,128]{2,1,0:T(8,128)S(1)},...) custom-call(s32[216]{0:T(256)S(4)} %get-tuple-element.23.list_i, ...), custom_call_target="tpu_custom_call", output_to_operand_aliasing={{1}: (9, {}), {2}: (10, {}), {3}: (11, {}), {4}: (12, {}), ... | custom-call | tf_op jit(solution)/shard_map/pallas_call | solution.py:341
  (2 shorter events, 0.0 us)
Async XLA Ops:
  0.0 7.1 %collective-permute-start.2 = (bf16[20,16,128]{2,1,0:T(8,128)(2,1)}, bf16[20,16,128]{2,1,0:T(8,128)(2,1)S(1)}, u32[]{:S(2)}, u32[]{:S(2)}) collective-permute-start(bf16[20,16,128]{2,1,0:T(8,128)(2,1)} %bitcast.7), channel_id=1, source_target_pairs={{0,2},{4,6},{8,10},{12,14},{2,0},{6,4},{10,8},{14,12},{1,3},{5,7},... | collective-permute-start | bytes 245768 | tf_op jit(solution)/shard_map/ppermute | solution.py:277
  4.0 3.1 %collective-permute-start.3 = (bf16[16,128]{1,0:T(8,128)(2,1)S(1)}, bf16[16,128]{1,0:T(8,128)(2,1)S(1)}, u32[]{:S(2)}, u32[]{:S(2)}) collective-permute-start(bf16[16,128]{1,0:T(8,128)(2,1)S(1)} %get-tuple-element.30), channel_id=1, source_target_pairs={{0,3},{1,2},{4,7},{5,6},{8,11},{9,10},{12,15},{13,14},{3,0},{2,1},... | collective-permute-start | bytes 12296 | tf_op jit(solution)/shard_map/ppermute | solution.py:277
  4.1 3.0 %collective-permute-start = (bf16[16,128]{1,0:T(8,128)(2,1)S(1)}, bf16[16,128]{1,0:T(8,128)(2,1)S(1)}, u32[]{:S(2)}, u32[]{:S(2)}) collective-permute-start(bf16[16,128]{1,0:T(8,128)(2,1)S(1)} %get-tuple-element.30), channel_id=1, source_target_pairs={{0,1},{1,0},{2,3},{3,2},{4,5},{5,4},{6,7},{7,6},{8,9},{9,8},{10,11... | collective-permute-start | bytes 12296 | tf_op jit(solution)/shard_map/ppermute | solution.py:277
  7.2 10.7 %collective-permute-start.5 = (bf16[42,16,128]{2,1,0:T(8,128)(2,1)S(1)}, bf16[42,16,128]{2,1,0:T(8,128)(2,1)S(1)}, u32[]{:S(2)}, u32[]{:S(2)}) collective-permute-start(bf16[42,16,128]{2,1,0:T(8,128)(2,1)S(1)} %pad_maximum_fusion), channel_id=1, source_target_pairs={{4,8},{6,10},{0,2},{12,14},{8,4},{10,6},{2,0},{14,12},{5,9},{7,11}... | collective-permute-start | bytes 516104 | tf_op jit(solution)/shard_map/ppermute | solution.py:277
  7.8 10.1 %collective-permute-start.4 = (bf16[42,16,128]{2,1,0:T(8,128)(2,1)S(1)}, bf16[42,16,128]{2,1,0:T(8,128)(2,1)S(1)}, u32[]{:S(2)}, u32[]{:S(2)}) collective-permute-start(bf16[42,16,128]{2,1,0:T(8,128)(2,1)S(1)} %pad_maximum_fusion), channel_id=1, source_target_pairs={{0,4},{2,6},{8,12},{10,14},{4,0},{6,2},{12,8},{14,10},{1,5},{3,7},... | collective-permute-start | bytes 516104 | tf_op jit(solution)/shard_map/ppermute | solution.py:277
  10.4 7.5 %collective-permute-start.1 = (bf16[21,16,128]{2,1,0:T(8,128)(2,1)S(1)}, bf16[21,16,128]{2,1,0:T(8,128)(2,1)S(1)}, u32[]{:S(2)}, u32[]{:S(2)}) collective-permute-start(bf16[21,16,128]{2,1,0:T(8,128)(2,1)S(1)} %pad_maximum_fusion.1), channel_id=1, source_target_pairs={{2,8},{6,12},{0,4},{10,14},{8,2},{12,6},{4,0},{14,10},{3,9},{7,13}... | collective-permute-start | bytes 258056 | tf_op jit(solution)/shard_map/ppermute | solution.py:277

commit v3 on v2

--- a/solution.py
+++ b/solution.py
@@ -31,59 +31,74 @@
     return block % 2, (block // 2) % 2, block // 2
 
 
-def select_kernel(pairs_ref, list_i, list_j, second, third, counts, band_ref, *, dates, unroll, local_cap):
+def select_kernel(
+    pairs_ref, list_i, list_j, second, third, counts, band_ref, of_first, of_second,
+    *, dates, size, unroll, mid_at, late_at,
+):
     cols = band_ref.shape[1]
-    odd, _, chip = place()
+    odd, far, chip = place()
     base = dates * (2 * chip - 3)
-    own = base + (3 + odd) * dates
-    inner = base + 3 * dates
     row = lax.broadcasted_iota(jnp.int32, band_ref.shape, 0)
     column = lax.broadcasted_iota(jnp.int32, band_ref.shape, 1)
     apart = jnp.where(row < cols, row, row - 2 * cols * lax.axis_index("pix")) - column
     band_ref[...] = jnp.where((apart <= WIN) & (apart >= -WIN), 1.0, 0.0).astype(band_ref.dtype)
 
-    def one(p, found):
-        near, other, n2, n3 = found
-        i, j = pairs_ref[0, p], pairs_ref[1, p]
-
-        def within(low, high):
-            return ((j >= low) & (i < high)).astype(jnp.int32)
-
-        local = ((i >= inner) & (j < inner + 2 * dates)).astype(jnp.int32)
-        where = jnp.where(local == 1, near, other)
-        list_i[where] = i - base
-        list_j[where] = j - base
-        second[n2] = where
-        third[n3] = where
-        return (
-            near + local,
-            other + (1 - local) * within(own - 2 * dates, own + 3 * dates),
-            n2 + within(own - dates, own + 2 * dates),
-            n3 + within(own, own + dates),
-        )
-
-    def four(q, found):
-        for u in range(4):
-            found = one(4 * q + u, found)
-        return found
+    def classify(block, carry):
+        slot = block - (2 * chip - 3)
+        away = slot - 3 - odd
+        near = jnp.where((slot == 3) | (slot == 4), 1, 0)
+        soon = jnp.where((slot == 1 + 4 * far) | (slot == 2 + 4 * far), 0, 2)
+        first = jnp.where(away <= 2, soon, 0) + near
+        second = jnp.where(away >= -2, soon, 0) + near
+        for reach in range(3):
+            first = first + jnp.where(away <= reach, 16 >> reach, 0)
+            second = second + jnp.where(away >= -reach, 16 >> reach, 0)
+        for k in range(dates):
+            of_first[block * dates + k] = first
+            of_second[block * dates + k] = second
+        return carry
+
+    lax.fori_loop(0, size, classify, 0)
+
+    def several(width):
+        def run(q, found):
+            at = [width * q + u for u in range(width)]
+            ends = [(pairs_ref[0, p], pairs_ref[1, p]) for p in at]
+            bits = [of_first[i] & of_second[j] for i, j in ends]
+            near, mid, late, n2, n3 = found
+            for (i, j), bit in zip(ends, bits, strict=True):
+                here, soon = bit & 1, (bit >> 1) & 1
+                where = jnp.where(here == 1, near, jnp.where(soon == 1, mid, late))
+                list_i[where] = i - base
+                list_j[where] = j - base
+                second[n2] = where
+                third[n3] = where
+                near = near + here
+                mid = mid + soon - here
+                late = late + ((bit >> 2) & 1) - soon
+                n2 = n2 + ((bit >> 3) & 1)
+                n3 = n3 + (bit >> 4)
+            return near, mid, late, n2, n3
+
+        return run
 
     zero = jnp.int32(0)
     total = pairs_ref.shape[1]
-    found = (zero, jnp.int32(local_cap), zero, zero)
-    found = lax.fori_loop(0, total // 4, four, found)
-    near, other, n2, n3 = lax.fori_loop(total // 4 * 4, total, one, found)
-    for u in range(SPARE * unroll):
-        list_i[near + u] = 8 * dates
-        list_j[near + u] = 8 * dates
-        list_i[other + u] = 8 * dates
-        list_j[other + u] = 8 * dates
+    found = (zero, jnp.int32(mid_at), jnp.int32(late_at), zero, zero)
+    found = lax.fori_loop(0, total // 8, several(8), found)
+    near, mid, late, n2, n3 = lax.fori_loop(total // 8 * 8, total, several(1), found)
+    for end in (near, mid, late):
+        for u in range(SPARE * unroll):
+            list_i[end + u] = 8 * dates
+            list_j[end + u] = 8 * dates
     for u in range(unroll):
-        second[n2 + u] = other
-        third[n3 + u] = other
+        second[n2 + u] = late
+        third[n3 + u] = late
     counts[0] = near
-    counts[1] = other - local_cap
-    counts[2] = n2
-    counts[3] = n3
+    counts[1] = mid - mid_at
+    counts[2] = late - late_at
+    counts[3] = n2
+    counts[4] = n3
 
 
 def make_boxes(rows, stage, band_ref):
@@ -205,9 +220,25 @@
     cohere(boxes, fields, (are, aim), list_i, list_j, cre, cim, 0, counts[0], batch)
 
 
+def mid_kernel(list_i, list_j, counts, band_ref, cross_ref, za_ref, *refs, batch, width, dates, mid_at):
+    sre, sim, hre, him, power, are, aim, cre, cim, stage = refs[9:]
+    _, rows, cols = sre.shape
+    tiles = 2 * dates + 1
+    odd, far, _ = place()
+    stage[...] = jnp.zeros_like(stage)
+    boxes = make_boxes(rows, stage, band_ref)
+    fields = (sre, sim, hre, him, power)
+    load = loader(dates, cols, width, boxes, fields)
+    up = 5 - 4 * far
+    load(cross_ref, 0, cross_ref[tiles - 1], 7 * odd * dates)
+    load(za_ref, 0, za_ref[tiles - 1], (up + odd) * dates)
+    load(za_ref, tiles, za_ref[2 * tiles - 1], (up + 1 - odd) * dates)
+    cohere(boxes, fields, (are, aim), list_i, list_j, cre, cim, mid_at, counts[1], batch)
+
+
 def link_kernel(
-    list_i, list_j, second, third, counts, band_ref, cross_ref, za_ref, zb_ref, *refs,
-    batch, unroll, width, local_cap,
+    list_i, list_j, second, third, counts, band_ref, zb_ref, *refs,
+    batch, unroll, width, late_at,
 ):
     out_ref, sre, sim, hre, him, power, are, aim, cre, cim, bre, bim, stage = refs[9:]
     _, dates, rows, cols = out_ref.shape
@@ -218,15 +249,11 @@
     boxes = make_boxes(rows, stage, band_ref)
     fields = (sre, sim, hre, him, power)
     load = loader(dates, cols, width, boxes, fields)
-    others, n2, n3 = counts[1], counts[2], counts[3]
-
-    load(cross_ref, 0, cross_ref[tiles - 1], 7 * odd * dates)
-    up, down = 5 - 4 * far, 1 + 4 * far
-    load(za_ref, 0, za_ref[tiles - 1], (up + odd) * dates)
-    load(za_ref, tiles, za_ref[2 * tiles - 1], (up + 1 - odd) * dates)
+    others, n2, n3 = counts[2], counts[3], counts[4]
+    down = 1 + 4 * far
     load(zb_ref, 0, zb_ref[tiles - 1], (down + odd) * dates)
     load(zb_ref, tiles, zb_ref[2 * tiles - 1], (down + 1 - odd) * dates)
-    cohere(boxes, fields, (are, aim), list_i, list_j, cre, cim, local_cap, others, batch)
+    cohere(boxes, fields, (are, aim), list_i, list_j, cre, cim, late_at, others, batch)
 
     def scaled(re, im):
         scale = lax.rsqrt(jnp.maximum(re * re + im * im, 1.0))
@@ -293,6 +320,7 @@
     def matching(step, keep):
         return [(i, i + step) for i in range(size - step) if keep(i)]
 
+    small = pltpu.CompilerParams(vmem_limit_bytes=4 * 1024 * 1024)
     main = slc.reshape(comps * dates, rows, cols)
     mates = matching(1, lambda i: i % 2 == 0)
     mate = swap(main, "date", mates)
@@ -301,6 +329,7 @@
         out_shape=[pltpu.VMEM(main.shape, slc.dtype), pltpu.VMEM((rows, cols), slc.dtype)],
         in_specs=[vmem],
         out_specs=[vmem] * 2,
+        compiler_params=small,
     )(main)
     edge_mine = swap(edge, "pix", [(0, 1)])
     edge_mate = swap(edge, ("date", "pix"), [(2 * i + p, 2 * j + 1 - p) for i, j in mates for p in (0, 1)])
@@ -314,19 +343,25 @@
     batch = max(1, 128 // rows)
     width = max(w for w in range(1, 2 * unroll + 1) if dates % w == 0)
     per_block = min(pair_count, 2 * pair_count // size)
-    local_cap = min(pair_count, 2 * per_block) + SPARE * unroll
-    cap = local_cap + min(pair_count, 6 * per_block) + SPARE * unroll
+    mid_at = min(pair_count, 2 * per_block) + SPARE * unroll
+    late_at = mid_at + min(pair_count, 4 * per_block) + SPARE * unroll
+    cap = late_at + min(pair_count, 4 * per_block) + SPARE * unroll
     window = 8 * dates + 1
     stage = pltpu.VMEM((16 + max(width, 4 * batch) * (rows + 8), cols), jnp.float32)
     plane = 4 * rows * cols
     spare = 4 * 1024 * 1024 + 64 * plane
-    lists = pl.pallas_call(
-        functools.partial(select_kernel, dates=dates, unroll=unroll, local_cap=local_cap),
-        out_shape=[pltpu.SMEM((n,), jnp.int32) for n in (cap, cap, pair_count + unroll, pair_count + unroll, 4)]
+    chosen = pl.pallas_call(
+        functools.partial(
+            select_kernel, dates=dates, size=size, unroll=unroll, mid_at=mid_at, late_at=late_at
+        ),
+        out_shape=[pltpu.SMEM((n,), jnp.int32) for n in (cap, cap, pair_count + unroll, pair_count + unroll, 5)]
         + [pltpu.VMEM((2 * cols, cols), jnp.bfloat16)],
         in_specs=[smem],
         out_specs=[smem] * 5 + [vmem],
-    )(pairs.T)
+        scratch_shapes=[pltpu.SMEM((size * dates,), jnp.int32)] * 2,
+        compiler_params=small,
+    )
+    lists = chosen(pairs.T)
     band = held(lists[5])
     lists = [pltpu.with_memory_space_constraint(v, pltpu.SMEM) for v in lists[:5]]
     fields = [pltpu.VMEM((window, rows, cols), jnp.float32)] * 7 + [pltpu.VMEM((cap, rows, cols), jnp.float32)] * 2
@@ -338,15 +373,24 @@
         scratch_shapes=[stage],
         compiler_params=pltpu.CompilerParams(vmem_limit_bytes=spare),
     )(lists[0], lists[1], lists[4], band, held(near), held(mate), held(edge_mine), held(edge_mate))
+    local = pl.pallas_call(
+        functools.partial(mid_kernel, batch=batch, width=width, dates=dates, mid_at=mid_at),
+        out_shape=fields,
+        in_specs=[smem] * 3 + [vmem] * 12,
+        out_specs=[vmem] * 9,
+        input_output_aliases={6 + k: k for k in range(9)},
+        scratch_shapes=[stage],
+        compiler_params=pltpu.CompilerParams(vmem_limit_bytes=spare),
+    )(lists[0], lists[1], lists[4], band, held(cross), held(za), *(held(v) for v in local))
     linked = pl.pallas_call(
-        functools.partial(link_kernel, batch=batch, unroll=unroll, width=width, local_cap=local_cap),
+        functools.partial(link_kernel, batch=batch, unroll=unroll, width=width, late_at=late_at),
         out_shape=[jax.ShapeDtypeStruct((comps, dates, rows, cols), jnp.float32), *fields],
-        in_specs=[smem] * 5 + [vmem] * 13,
+        in_specs=[smem] * 5 + [vmem] * 11,
         out_specs=[vmem] * 10,
-        input_output_aliases={9 + k: 1 + k for k in range(9)},
+        input_output_aliases={7 + k: 1 + k for k in range(9)},
         scratch_shapes=[fields[0]] * 2 + [stage],
         compiler_params=pltpu.CompilerParams(vmem_limit_bytes=spare + 2 * window * plane),
-    )(*lists, band, held(cross), held(za), held(zb), *(held(v) for v in local))
+    )(*lists, band, held(zb), *(held(v) for v in local))
     return linked[0]
 
 

time: 21.1 us -> 21.6 us (1.024)
  the two profiles are of different devices: /device:TPU:0 before, /device:TPU:4 now
where the time goes in v3:
time: 21.6 us; the launch traced here: 21.4 us
  Pallas kernels  8.01 us (37%)
  starting transfers between devices  7.4 us (34%)
  waiting for transfers between devices  4.31 us (20%)
  local copies, waits for them, and re-layouts  1.6 us (7%)
    ppermute x6, starting transfers between devices, swap(): return lax.ppermute(array, axis, [*pairing, *((j, i) for i, j in pairing)])  7.4 us
    ppermute x6, waiting for transfers between devices, swap(): return lax.ppermute(array, axis, [*pairing, *((j, i) for i, j in pairing)])  4.31 us
    pallas_call x1, Pallas kernels, on_device(): lists = chosen(pairs.T)  2.5 us
    pallas_call x1, Pallas kernels, on_device(): pl.pallas_call(functools.partial(link_kernel, batch=batch, unroll=unroll,...  2.26 us
    pallas_call x1, Pallas kernels, on_device(): pl.pallas_call(functools.partial(mid_kernel, batch=batch, width=width, da...  1.78 us
    unnamed x4, local copies, waits for them, and re-layouts  1.6 us
    pallas_call x1, Pallas kernels, on_device(): pl.pallas_call(functools.partial(near_kernel, dates=dates, batch=batch, w...  1.37 us
  transfers between devices with their start and end apart: 6, of which 3 were waited for; matrix products, arithmetic and copies ran while one was open for 0% of the time, Pallas kernels for 27%

profile of v3, /device:TPU:4, one launch (start us, length us, event | category | flops | bytes accessed | tf_op | source)
XLA Modules:
  0.0 21.4 jit_solution(12348359020039525421)
XLA Ops:
  0.0 0.0 collective-permute-start.1
  0.0 0.0 copy-start
  0.0 0.9 %copy-done = bf16[2,10,16,128]{3,2,1,0:T(8,128)(2,1)S(1)} copy-done((bf16[2,10,16,128]{3,2,1,0:T(8,128)(2,1)S(1)}, bf16[2,10,16,128]{3,2,1,0:T(8,128)(2,1)}, u32[]{:S(2)}) %copy-start) | copy-done | bytes 81944
  0.9 0.1 shard_map.29
  1.0 1.2 %collective-permute-start.2 = (bf16[16,128]{1,0:T(8,128)(2,1)S(1)}, bf16[16,128]{1,0:T(8,128)(2,1)S(1)}, u32[]{:S(2)}, u32[]{:S(2)}) collective-permute-start(bf16[16,128]{1,0:T(8,128)(2,1)S(1)} %get-tuple-element.39), channel_id=1, source_target_pairs={{0,3},{1,2},{4,7},{5,6},{8,11},{9,10},{12,15},{13,14},{3,0},{2,1},... | collective-permute-start | bytes 12296 | tf_op jit(solution)/shard_map/ppermute | solution.py:304
  2.3 1.0 %collective-permute-start = (bf16[16,128]{1,0:T(8,128)(2,1)S(1)}, bf16[16,128]{1,0:T(8,128)(2,1)S(1)}, u32[]{:S(2)}, u32[]{:S(2)}) collective-permute-start(bf16[16,128]{1,0:T(8,128)(2,1)S(1)} %get-tuple-element.39), channel_id=1, source_target_pairs={{0,1},{1,0},{2,3},{3,2},{4,5},{5,4},{6,7},{7,6},{8,9},{9,8},{10,11... | collective-permute-start | bytes 12296 | tf_op jit(solution)/shard_map/ppermute | solution.py:304
  3.2 0.9 %collective-permute-done.2.edge_mate_ref = bf16[16,128]{1,0:T(8,128)(2,1)S(1)} collective-permute-done((bf16[16,128]{1,0:T(8,128)(2,1)S(1)}, bf16[16,128]{1,0:T(8,128)(2,1)S(1)}, u32[]{:S(2)}, u32[]{:S(2)}) %collective-permute-start.2) | collective-permute-done | bytes 4128 | tf_op jit(solution)/shard_map/ppermute | solution.py:304
  4.2 0.0 collective-permute-done.edge_mine_ref
  4.2 0.5 %collective-permute-done.1.mate_ref = bf16[20,16,128]{2,1,0:T(8,128)(2,1)S(1)} collective-permute-done((bf16[20,16,128]{2,1,0:T(8,128)(2,1)}, bf16[20,16,128]{2,1,0:T(8,128)(2,1)S(1)}, u32[]{:S(2)}, u32[]{:S(2)}) %collective-permute-start.1) | collective-permute-done | bytes 81952 | tf_op jit(solution)/shard_map/ppermute | solution.py:304
  4.7 1.6 %collective-permute-start.5 = (bf16[42,16,128]{2,1,0:T(8,128)(2,1)S(1)}, bf16[42,16,128]{2,1,0:T(8,128)(2,1)S(1)}, u32[]{:S(2)}, u32[]{:S(2)}) collective-permute-start(bf16[42,16,128]{2,1,0:T(8,128)(2,1)S(1)} %pad_maximum_fusion), channel_id=1, source_target_pairs={{0,4},{2,6},{8,12},{10,14},{4,0},{6,2},{12,8},{14,10},{1,5},{3,7},... | collective-permute-start | bytes 516104 | tf_op jit(solution)/shard_map/ppermute | solution.py:304
  6.4 1.5 %collective-permute-start.3 = (bf16[42,16,128]{2,1,0:T(8,128)(2,1)S(1)}, bf16[42,16,128]{2,1,0:T(8,128)(2,1)S(1)}, u32[]{:S(2)}, u32[]{:S(2)}) collective-permute-start(bf16[42,16,128]{2,1,0:T(8,128)(2,1)S(1)} %pad_maximum_fusion), channel_id=1, source_target_pairs={{4,8},{6,10},{0,2},{12,14},{8,4},{10,6},{2,0},{14,12},{5,9},{7,11}... | collective-permute-start | bytes 516104 | tf_op jit(solution)/shard_map/ppermute | solution.py:304
  7.8 2.1 %collective-permute-start.4 = (bf16[21,16,128]{2,1,0:T(8,128)(2,1)S(1)}, bf16[21,16,128]{2,1,0:T(8,128)(2,1)S(1)}, u32[]{:S(2)}, u32[]{:S(2)}) collective-permute-start(bf16[21,16,128]{2,1,0:T(8,128)(2,1)S(1)} %pad_maximum_fusion.1), channel_id=1, source_target_pairs={{2,8},{6,12},{0,4},{10,14},{8,2},{12,6},{4,0},{14,10},{3,9},{7,13}... | collective-permute-start | bytes 258056 | tf_op jit(solution)/shard_map/ppermute | solution.py:304
  9.9 0.0 copy-start.1
  9.9 0.7 %copy-done.1 = s32[112,2]{0,1:T(2,128)S(1)} copy-done((s32[112,2]{0,1:T(2,128)S(1)}, s32[112,2]{0,1:T(2,128)}, u32[]{:S(2)}) %copy-start.1) | copy-done | bytes 920
  10.6 2.5 %shard_map.28 = (s32[352]{0:T(512)S(4)}, s32[352]{0:T(512)S(4)}, s32[120]{0:T(128)S(4)}, s32[120]{0:T(128)S(4)}, s32[5]{0:T(128)S(4)}, /*index=5*/bf16[256,128]{1,0:T(8,128)(2,1)S(1)}) custom-call(s32[2,112]{1,0:T(2,128)S(1)} %bitcast.9), custom_call_target="tpu_custom_call" | custom-call | tf_op jit(solution)/shard_map/pallas_call | solution.py:364
  13.1 1.4 %shard_map.30 = (f32[81,16,128]{2,1,0:T(8,128)S(1)}, f32[81,16,128]{2,1,0:T(8,128)S(1)}, f32[81,16,128]{2,1,0:T(8,128)S(1)}, f32[81,16,128]{2,1,0:T(8,128)S(1)},...) custom-call(s32[352]{0:T(512)S(4)} %get-tuple-element.32.list_i, ...), custom_call_target="tpu_custom_call" | custom-call | tf_op jit(solution)/shard_map/pallas_call | solution.py:368
  14.5 2.8 %collective-permute-done.4.cross_ref = bf16[21,16,128]{2,1,0:T(8,128)(2,1)S(1)} collective-permute-done((bf16[21,16,128]{2,1,0:T(8,128)(2,1)S(1)}, bf16[21,16,128]{2,1,0:T(8,128)(2,1)S(1)}, u32[]{:S(2)}, u32[]{:S(2)}) %collective-permute-start.4) | collective-permute-done | bytes 86048 | tf_op jit(solution)/shard_map/ppermute | solution.py:304
  17.4 0.0 collective-permute-done.5.za_ref
  17.4 1.8 %shard_map.31 = (f32[81,16,128]{2,1,0:T(8,128)S(1)}, f32[81,16,128]{2,1,0:T(8,128)S(1)}, f32[81,16,128]{2,1,0:T(8,128)S(1)}, f32[81,16,128]{2,1,0:T(8,128)S(1)},...) custom-call(s32[352]{0:T(512)S(4)} %get-tuple-element.32.list_i, ...), custom_call_target="tpu_custom_call", output_to_operand_aliasing={{0}: (6, {}), {1}: (7, {}), {2}: (8, {}), {3}: (9, {}), {4}... | custom-call | tf_op jit(solution)/shard_map/pallas_call | solution.py:376
  19.1 0.0 collective-permute-done.3.zb_ref
  19.2 2.3 %shard_map.32 = (f32[2,10,16,128]{3,2,1,0:T(8,128)}, f32[81,16,128]{2,1,0:T(8,128)S(1)}, f32[81,16,128]{2,1,0:T(8,128)S(1)}, f32[81,16,128]{2,1,0:T(8,128)S(1)},...) custom-call(s32[352]{0:T(512)S(4)} %get-tuple-element.32.list_i, ...), custom_call_target="tpu_custom_call", output_to_operand_aliasing={{1}: (7, {}), {2}: (8, {}), {3}: (9, {}), {4}: (10, {}), {5... | custom-call | tf_op jit(solution)/shard_map/pallas_call | solution.py:385
  (2 shorter events, 0.0 us)
Async XLA Ops:
  0.0 4.7 %collective-permute-start.1 = (bf16[20,16,128]{2,1,0:T(8,128)(2,1)}, bf16[20,16,128]{2,1,0:T(8,128)(2,1)S(1)}, u32[]{:S(2)}, u32[]{:S(2)}) collective-permute-start(bf16[20,16,128]{2,1,0:T(8,128)(2,1)} %bitcast.4), channel_id=1, source_target_pairs={{0,2},{4,6},{8,10},{12,14},{2,0},{6,4},{10,8},{14,12},{1,3},{5,7},... | collective-permute-start | bytes 245768 | tf_op jit(solution)/shard_map/ppermute | solution.py:304
  0.0 0.9 %copy-start = (bf16[2,10,16,128]{3,2,1,0:T(8,128)(2,1)S(1)}, bf16[2,10,16,128]{3,2,1,0:T(8,128)(2,1)}, u32[]{:S(2)}) copy-start(bf16[2,10,16,128]{3,2,1,0:T(8,128)(2,1)} %param.2) | copy-start | bytes 245764
  1.0 3.1 %collective-permute-start.2 = (bf16[16,128]{1,0:T(8,128)(2,1)S(1)}, bf16[16,128]{1,0:T(8,128)(2,1)S(1)}, u32[]{:S(2)}, u32[]{:S(2)}) collective-permute-start(bf16[16,128]{1,0:T(8,128)(2,1)S(1)} %get-tuple-element.39), channel_id=1, source_target_pairs={{0,3},{1,2},{4,7},{5,6},{8,11},{9,10},{12,15},{13,14},{3,0},{2,1},... | collective-permute-start | bytes 12296 | tf_op jit(solution)/shard_map/ppermute | solution.py:304
  2.3 1.9 %collective-permute-start = (bf16[16,128]{1,0:T(8,128)(2,1)S(1)}, bf16[16,128]{1,0:T(8,128)(2,1)S(1)}, u32[]{:S(2)}, u32[]{:S(2)}) collective-permute-start(bf16[16,128]{1,0:T(8,128)(2,1)S(1)} %get-tuple-element.39), channel_id=1, source_target_pairs={{0,1},{1,0},{2,3},{3,2},{4,5},{5,4},{6,7},{7,6},{8,9},{9,8},{10,11... | collective-permute-start | bytes 12296 | tf_op jit(solution)/shard_map/ppermute | solution.py:304
  4.7 12.6 %collective-permute-start.5 = (bf16[42,16,128]{2,1,0:T(8,128)(2,1)S(1)}, bf16[42,16,128]{2,1,0:T(8,128)(2,1)S(1)}, u32[]{:S(2)}, u32[]{:S(2)}) collective-permute-start(bf16[42,16,128]{2,1,0:T(8,128)(2,1)S(1)} %pad_maximum_fusion), channel_id=1, source_target_pairs={{0,4},{2,6},{8,12},{10,14},{4,0},{6,2},{12,8},{14,10},{1,5},{3,7},... | collective-permute-start | bytes 516104 | tf_op jit(solution)/shard_map/ppermute | solution.py:304
  6.4 12.8 %collective-permute-start.3 = (bf16[42,16,128]{2,1,0:T(8,128)(2,1)S(1)}, bf16[42,16,128]{2,1,0:T(8,128)(2,1)S(1)}, u32[]{:S(2)}, u32[]{:S(2)}) collective-permute-start(bf16[42,16,128]{2,1,0:T(8,128)(2,1)S(1)} %pad_maximum_fusion), channel_id=1, source_target_pairs={{4,8},{6,10},{0,2},{12,14},{8,4},{10,6},{2,0},{14,12},{5,9},{7,11}... | collective-permute-start | bytes 516104 | tf_op jit(solution)/shard_map/ppermute | solution.py:304
  7.8 9.5 %collective-permute-start.4 = (bf16[21,16,128]{2,1,0:T(8,128)(2,1)S(1)}, bf16[21,16,128]{2,1,0:T(8,128)(2,1)S(1)}, u32[]{:S(2)}, u32[]{:S(2)}) collective-permute-start(bf16[21,16,128]{2,1,0:T(8,128)(2,1)S(1)} %pad_maximum_fusion.1), channel_id=1, source_target_pairs={{2,8},{6,12},{0,4},{10,14},{8,2},{12,6},{4,0},{14,10},{3,9},{7,13}... | collective-permute-start | bytes 258056 | tf_op jit(solution)/shard_map/ppermute | solution.py:304
  9.9 0.7 %copy-start.1 = (s32[112,2]{0,1:T(2,128)S(1)}, s32[112,2]{0,1:T(2,128)}, u32[]{:S(2)}) copy-start(s32[112,2]{0,1:T(2,128)} %param.3) | copy-start | bytes 2692

commit v4 on v3

--- a/solution.py
+++ b/solution.py
@@ -31,74 +31,72 @@
     return block % 2, (block // 2) % 2, block // 2
 
 
-def select_kernel(
-    pairs_ref, list_i, list_j, second, third, counts, band_ref, of_first, of_second,
-    *, dates, size, unroll, mid_at, late_at,
-):
+def select_kernel(pairs_ref, *refs, dates, mid_at, late_at, cap):
+    outs, band_ref, padded, staged, sems = refs[:5], refs[5], refs[6], refs[7:12], refs[12]
     cols = band_ref.shape[1]
     odd, far, chip = place()
-    base = dates * (2 * chip - 3)
+    own, inner, last = (3 + odd) * dates, 3 * dates, (1 + 4 * far) * dates
     row = lax.broadcasted_iota(jnp.int32, band_ref.shape, 0)
     column = lax.broadcasted_iota(jnp.int32, band_ref.shape, 1)
     apart = jnp.where(row < cols, row, row - 2 * cols * lax.axis_index("pix")) - column
     band_ref[...] = jnp.where((apart <= WIN) & (apart >= -WIN), 1.0, 0.0).astype(band_ref.dtype)
 
-    def classify(block, carry):
-        slot = block - (2 * chip - 3)
-        away = slot - 3 - odd
-        near = jnp.where((slot == 3) | (slot == 4), 1, 0)
-        soon = jnp.where((slot == 1 + 4 * far) | (slot == 2 + 4 * far), 0, 2)
-        first = jnp.where(away <= 2, soon, 0) + near
-        second = jnp.where(away >= -2, soon, 0) + near
-        for reach in range(3):
-            first = first + jnp.where(away <= reach, 16 >> reach, 0)
-            second = second + jnp.where(away >= -reach, 16 >> reach, 0)
-        for k in range(dates):
-            of_first[block * dates + k] = first
-            of_second[block * dates + k] = second
-        return carry
-
-    lax.fori_loop(0, size, classify, 0)
-
-    def several(width):
-        def run(q, found):
-            at = [width * q + u for u in range(width)]
-            ends = [(pairs_ref[0, p], pairs_ref[1, p]) for p in at]
-            bits = [of_first[i] & of_second[j] for i, j in ends]
-            near, mid, late, n2, n3 = found
-            for (i, j), bit in zip(ends, bits, strict=True):
-                here, soon = bit & 1, (bit >> 1) & 1
-                where = jnp.where(here == 1, near, jnp.where(soon == 1, mid, late))
-                list_i[where] = i - base
-                list_j[where] = j - base
-                second[n2] = where
-                third[n3] = where
-                near = near + here
-                mid = mid + soon - here
-                late = late + ((bit >> 2) & 1) - soon
-                n2 = n2 + ((bit >> 3) & 1)
-                n3 = n3 + (bit >> 4)
-            return near, mid, late, n2, n3
-
-        return run
-
-    zero = jnp.int32(0)
-    total = pairs_ref.shape[1]
-    found = (zero, jnp.int32(mid_at), jnp.int32(late_at), zero, zero)
-    found = lax.fori_loop(0, total // 8, several(8), found)
-    near, mid, late, n2, n3 = lax.fori_loop(total // 8 * 8, total, several(1), found)
-    for end in (near, mid, late):
-        for u in range(SPARE * unroll):
-            list_i[end + u] = 8 * dates
-            list_j[end + u] = 8 * dates
-    for u in range(unroll):
-        second[n2 + u] = late
-        third[n3 + u] = late
-    counts[0] = near
-    counts[1] = mid - mid_at
-    counts[2] = late - late_at
-    counts[3] = n2
-    counts[4] = n3
+    lanes, length = padded.shape[1], staged[0].shape[1]
+    padded[...] = jnp.full(padded.shape, -(2**20), jnp.int32)
+    padded[pl.ds(0, 2), pl.ds(0, pairs_ref.shape[1])] = pairs_ref[...]
+    dated = padded[...] - dates * (2 * chip - 3)
+    i, j = dated[0:1], dated[1:2]
+
+    def flag(condition):
+        return jnp.where(condition, 1.0, 0.0)
+
+    def within(reach):
+        return flag(j >= own - reach * dates) * flag(i < own + (reach + 1) * dates)
+
+    def absent(date):
+        return 1.0 - flag(date >= last) * flag(date < last + 2 * dates)
+
+    near = flag(i >= inner) * flag(j < inner + 2 * dates)
+    wanted = within(2)
+    soon = wanted * absent(i) * absent(j)
+    classes = [near, soon - near, wanted - soon, within(1), within(0)]
+    empty = jnp.zeros((1, lanes), jnp.float32)
+    stack = jnp.concatenate([*classes, empty, empty, empty], axis=0)
+    before = flag(
+        lax.broadcasted_iota(jnp.int32, (lanes, lanes), 0) < lax.broadcasted_iota(jnp.int32, (lanes, lanes), 1)
+    ).astype(jnp.bfloat16)
+    ranks = jnp.dot(stack.astype(jnp.bfloat16), before, preferred_element_type=jnp.float32)
+    rank = [ranks[k : k + 1] for k in range(5)]
+    where = classes[0] * rank[0] + classes[1] * (rank[1] + mid_at) + classes[2] * (rank[2] + late_at)
+    targets = [where + wanted - 1.0, classes[3] * (rank[3] + 1.0) - 1.0, classes[4] * (rank[4] + 1.0) - 1.0]
+    upright = jnp.transpose(jnp.concatenate([*targets, *[empty] * 5], axis=0))
+    slots = lax.broadcasted_iota(jnp.int32, (lanes, length), 1).astype(jnp.float32)
+    ones = jnp.ones((1, lanes), jnp.float32)
+    upper = jnp.floor(where * (1.0 / 128.0))
+
+    def scatter(k, values):
+        hot = flag(upright[:, k : k + 1] == slots).astype(jnp.bfloat16)
+        rows = jnp.concatenate([*values, *[empty] * (8 - len(values))], axis=0).astype(jnp.bfloat16)
+        return jnp.dot(rows, hot, preferred_element_type=jnp.float32)
+
+    ends = scatter(0, [i.astype(jnp.float32) * wanted, j.astype(jnp.float32) * wanted, ones])
+    free = 8.0 * dates * (1.0 - ends[2:3])
+    staged[0][...] = (ends[0:1] + free).astype(jnp.int32)
+    staged[1][...] = (ends[1:2] + free).astype(jnp.int32)
+    for k in (1, 2):
+        index = scatter(k, [upper, where - 128.0 * upper, ones])
+        spot = 128.0 * index[0:1] + index[1:2] + (cap - 1.0) * (1.0 - index[2:3])
+        staged[1 + k][...] = spot.astype(jnp.int32)
+    sums = jnp.broadcast_to(jnp.sum(stack, axis=1, keepdims=True), (8, length))
+    own_lane = flag(
+        lax.broadcasted_iota(jnp.int32, (8, length), 0) == lax.broadcasted_iota(jnp.int32, (8, length), 1)
+    )
+    staged[4][...] = jnp.sum(sums * own_lane, axis=0, keepdims=True).astype(jnp.int32)
+    copies = [pltpu.make_async_copy(staged[k], outs[k], sems.at[k]) for k in range(5)]
+    for copy in copies:
+        copy.start()
+    for copy in copies:
+        copy.wait()
 
 
 def make_boxes(rows, stage, band_ref):
@@ -164,7 +162,7 @@
         centers, halos = [], []
         for u in range(width):
             p = first + group * width + u
-            i, j = list_i[p], list_j[p]
+            i, j = list_i[0, p], list_j[0, p]
             centers += cross(sre[i], sim[i], sre[j], sim[j])
             halos += cross(hre[i], him[i], hre[j], him[j])
         spread(centers, halos, 2 * width * half)
@@ -172,7 +170,7 @@
     def finish(group, half):
         for u in range(width):
             p = first + group * width + u
-            i, j = list_i[p], list_j[p]
+            i, j = list_i[0, p], list_j[0, p]
             scale = 2.0 / (power[i] + power[j])
             slot = 2 * (width * half + u)
             re, im = gather(slot) * scale, gather(slot + 1) * scale
@@ -217,7 +215,7 @@
     load(mate_ref, 0, edge_mate_ref[...], (4 - odd) * dates)
     are[...] = jnp.ones_like(are)
     aim[...] = jnp.zeros_like(aim)
-    cohere(boxes, fields, (are, aim), list_i, list_j, cre, cim, 0, counts[0], batch)
+    cohere(boxes, fields, (are, aim), list_i, list_j, cre, cim, 0, counts[0, 0], batch)
 
 
 def mid_kernel(list_i, list_j, counts, band_ref, cross_ref, za_ref, *refs, batch, width, dates, mid_at):
@@ -233,7 +231,7 @@
     load(cross_ref, 0, cross_ref[tiles - 1], 7 * odd * dates)
     load(za_ref, 0, za_ref[tiles - 1], (up + odd) * dates)
     load(za_ref, tiles, za_ref[2 * tiles - 1], (up + 1 - odd) * dates)
-    cohere(boxes, fields, (are, aim), list_i, list_j, cre, cim, mid_at, counts[1], batch)
+    cohere(boxes, fields, (are, aim), list_i, list_j, cre, cim, mid_at, counts[0, 1], batch)
 
 
 def link_kernel(
@@ -249,7 +247,7 @@
     boxes = make_boxes(rows, stage, band_ref)
     fields = (sre, sim, hre, him, power)
     load = loader(dates, cols, width, boxes, fields)
-    others, n2, n3 = counts[2], counts[3], counts[4]
+    others, n2, n3 = counts[0, 2], counts[0, 3], counts[0, 4]
     down = 1 + 4 * far
     load(zb_ref, 0, zb_ref[tiles - 1], (down + odd) * dates)
     load(zb_ref, tiles, zb_ref[2 * tiles - 1], (down + 1 - odd) * dates)
@@ -275,8 +273,8 @@
     def step(index, count, xr, xi, yr, yi):
         def several(first):
             for u in range(unroll):
-                p = index[first + u]
-                i, j = list_i[p], list_j[p]
+                p = index[0, first + u]
+                i, j = list_i[0, p], list_j[0, p]
                 re, im = cre[p], cim[p]
                 nr, ni, fr, fi = xr[i], xi[i], xr[j], xi[j]
                 ri, rj, ii, ij = yr[i], yr[j], yi[i], yi[j]
@@ -350,15 +348,16 @@
     stage = pltpu.VMEM((16 + max(width, 4 * batch) * (rows + 8), cols), jnp.float32)
     plane = 4 * rows * cols
     spare = 4 * 1024 * 1024 + 64 * plane
+    length = -(-max(cap, pair_count + unroll) // LANES) * LANES
+    lanes = -(-pair_count // LANES) * LANES
     chosen = pl.pallas_call(
-        functools.partial(
-            select_kernel, dates=dates, size=size, unroll=unroll, mid_at=mid_at, late_at=late_at
-        ),
-        out_shape=[pltpu.SMEM((n,), jnp.int32) for n in (cap, cap, pair_count + unroll, pair_count + unroll, 5)]
-        + [pltpu.VMEM((2 * cols, cols), jnp.bfloat16)],
-        in_specs=[smem],
+        functools.partial(select_kernel, dates=dates, mid_at=mid_at, late_at=late_at, cap=cap),
+        out_shape=[pltpu.SMEM((1, length), jnp.int32)] * 5 + [pltpu.VMEM((2 * cols, cols), jnp.bfloat16)],
+        in_specs=[vmem],
         out_specs=[smem] * 5 + [vmem],
-        scratch_shapes=[pltpu.SMEM((size * dates,), jnp.int32)] * 2,
+        scratch_shapes=[pltpu.VMEM((8, lanes), jnp.int32)]
+        + [pltpu.VMEM((1, length), jnp.int32)] * 5
+        + [pltpu.SemaphoreType.DMA((5,))],
         compiler_params=small,
     )
     lists = chosen(pairs.T)
@@ -398,6 +397,4 @@
     in_specs = (P(None, ("grp", "date"), None, "pix"), P("grp", None))
     out_specs = P(None, ("grp", "date"), None, "pix")
 
-    return jax.shard_map(
-        on_device, mesh=mesh, in_specs=in_specs, out_specs=out_specs, check_vma=False
-    )
+    return jax.shard_map(on_device, mesh=mesh, in_specs=in_specs, out_specs=out_specs, check_vma=False)

time: 21.6 us -> 21.6 us (level)
  waiting for transfers between devices: 4.31 us -> 5.64 us
  Pallas kernels: 8.01 us -> 6.69 us
    pallas_call x1, Pallas kernels: 2.5 us -> 1.18 us  [on_device(): lists = chosen(pairs.T)]
    ppermute x6, waiting for transfers between devices: 4.31 us -> 5.64 us  [swap(): return lax.ppermute(array, axis, [*pairing, *((j, i) for i, j in pairing)])]
  transfers between devices with their start and end apart: 6 -> 6, of which waited for: 3 -> 3; matrix products, arithmetic and copies ran while one was open for 0% -> 0% of each run, Pallas kernels for 27% -> 21%
where the time goes in v4:
time: 21.6 us; the launch traced here: 21.4 us
  starting transfers between devices  7.4 us (34%)
  Pallas kernels  6.69 us (31%)
  waiting for transfers between devices  5.64 us (26%)
  local copies, waits for them, and re-layouts  1.6 us (7%)
    ppermute x6, starting transfers between devices, swap(): return lax.ppermute(array, axis, [*pairing, *((j, i) for i, j in pairing)])  7.4 us
    ppermute x6, waiting for transfers between devices, swap(): return lax.ppermute(array, axis, [*pairing, *((j, i) for i, j in pairing)])  5.64 us
    pallas_call x1, Pallas kernels, on_device(): pl.pallas_call(functools.partial(link_kernel, batch=batch, unroll=unroll,...  2.26 us
    pallas_call x1, Pallas kernels, on_device(): pl.pallas_call(functools.partial(mid_kernel, batch=batch, width=width, da...  1.78 us
    unnamed x4, local copies, waits for them, and re-layouts  1.6 us
    pallas_call x1, Pallas kernels, on_device(): pl.pallas_call(functools.partial(near_kernel, dates=dates, batch=batch, w...  1.37 us
    pallas_call x1, Pallas kernels, on_device(): lists = chosen(pairs.T)  1.18 us
  transfers between devices with their start and end apart: 6, of which 3 were waited for; matrix products, arithmetic and copies ran while one was open for 0% of the time, Pallas kernels for 21%

profile of v4, /device:TPU:4, one launch (start us, length us, event | category | flops | bytes accessed | tf_op | source)
XLA Modules:
  0.0 21.4 jit_solution(14616755776831474808)
XLA Ops:
  0.0 0.0 collective-permute-start.1
  0.0 0.0 copy-start
  0.0 0.9 %copy-done = bf16[2,10,16,128]{3,2,1,0:T(8,128)(2,1)S(1)} copy-done((bf16[2,10,16,128]{3,2,1,0:T(8,128)(2,1)S(1)}, bf16[2,10,16,128]{3,2,1,0:T(8,128)(2,1)}, u32[]{:S(2)}) %copy-start) | copy-done | bytes 81944
  0.9 0.1 shard_map.29
  1.0 1.2 %collective-permute-start.2 = (bf16[16,128]{1,0:T(8,128)(2,1)S(1)}, bf16[16,128]{1,0:T(8,128)(2,1)S(1)}, u32[]{:S(2)}, u32[]{:S(2)}) collective-permute-start(bf16[16,128]{1,0:T(8,128)(2,1)S(1)} %get-tuple-element.39), channel_id=1, source_target_pairs={{0,3},{1,2},{4,7},{5,6},{8,11},{9,10},{12,15},{13,14},{3,0},{2,1},... | collective-permute-start | bytes 12296 | tf_op jit(solution)/shard_map/ppermute | solution.py:302
  2.3 1.0 %collective-permute-start = (bf16[16,128]{1,0:T(8,128)(2,1)S(1)}, bf16[16,128]{1,0:T(8,128)(2,1)S(1)}, u32[]{:S(2)}, u32[]{:S(2)}) collective-permute-start(bf16[16,128]{1,0:T(8,128)(2,1)S(1)} %get-tuple-element.39), channel_id=1, source_target_pairs={{0,1},{1,0},{2,3},{3,2},{4,5},{5,4},{6,7},{7,6},{8,9},{9,8},{10,11... | collective-permute-start | bytes 12296 | tf_op jit(solution)/shard_map/ppermute | solution.py:302
  3.2 0.9 %collective-permute-done.2.edge_mate_ref = bf16[16,128]{1,0:T(8,128)(2,1)S(1)} collective-permute-done((bf16[16,128]{1,0:T(8,128)(2,1)S(1)}, bf16[16,128]{1,0:T(8,128)(2,1)S(1)}, u32[]{:S(2)}, u32[]{:S(2)}) %collective-permute-start.2) | collective-permute-done | bytes 4128 | tf_op jit(solution)/shard_map/ppermute | solution.py:302
  4.2 0.0 collective-permute-done.edge_mine_ref
  4.2 0.5 %collective-permute-done.1.mate_ref = bf16[20,16,128]{2,1,0:T(8,128)(2,1)S(1)} collective-permute-done((bf16[20,16,128]{2,1,0:T(8,128)(2,1)}, bf16[20,16,128]{2,1,0:T(8,128)(2,1)S(1)}, u32[]{:S(2)}, u32[]{:S(2)}) %collective-permute-start.1) | collective-permute-done | bytes 81952 | tf_op jit(solution)/shard_map/ppermute | solution.py:302
  4.7 1.6 %collective-permute-start.5 = (bf16[42,16,128]{2,1,0:T(8,128)(2,1)S(1)}, bf16[42,16,128]{2,1,0:T(8,128)(2,1)S(1)}, u32[]{:S(2)}, u32[]{:S(2)}) collective-permute-start(bf16[42,16,128]{2,1,0:T(8,128)(2,1)S(1)} %pad_maximum_fusion), channel_id=1, source_target_pairs={{0,4},{2,6},{8,12},{10,14},{4,0},{6,2},{12,8},{14,10},{1,5},{3,7},... | collective-permute-start | bytes 516104 | tf_op jit(solution)/shard_map/ppermute | solution.py:302
  6.4 1.5 %collective-permute-start.3 = (bf16[42,16,128]{2,1,0:T(8,128)(2,1)S(1)}, bf16[42,16,128]{2,1,0:T(8,128)(2,1)S(1)}, u32[]{:S(2)}, u32[]{:S(2)}) collective-permute-start(bf16[42,16,128]{2,1,0:T(8,128)(2,1)S(1)} %pad_maximum_fusion), channel_id=1, source_target_pairs={{4,8},{6,10},{0,2},{12,14},{8,4},{10,6},{2,0},{14,12},{5,9},{7,11}... | collective-permute-start | bytes 516104 | tf_op jit(solution)/shard_map/ppermute | solution.py:302
  7.8 2.1 %collective-permute-start.4 = (bf16[21,16,128]{2,1,0:T(8,128)(2,1)S(1)}, bf16[21,16,128]{2,1,0:T(8,128)(2,1)S(1)}, u32[]{:S(2)}, u32[]{:S(2)}) collective-permute-start(bf16[21,16,128]{2,1,0:T(8,128)(2,1)S(1)} %pad_maximum_fusion.1), channel_id=1, source_target_pairs={{2,8},{6,12},{0,4},{10,14},{8,2},{12,6},{4,0},{14,10},{3,9},{7,13}... | collective-permute-start | bytes 258056 | tf_op jit(solution)/shard_map/ppermute | solution.py:302
  9.9 0.0 copy-start.1
  9.9 0.7 %copy-done.1 = s32[112,2]{0,1:T(2,128)S(1)} copy-done((s32[112,2]{0,1:T(2,128)S(1)}, s32[112,2]{0,1:T(2,128)}, u32[]{:S(2)}) %copy-start.1) | copy-done | bytes 920
  10.6 1.2 %shard_map.28 = (s32[1,384]{1,0:T(1,128)S(4)}, s32[1,384]{1,0:T(1,128)S(4)}, s32[1,384]{1,0:T(1,128)S(4)}, s32[1,384]{1,0:T(1,128)S(4)}, s32[1,384]{1,0:T(1,128)S(4)}, /*index=5*/bf16[256,128]{1,0:T(8,128)(2,1)S(1)}) custom-call(s32[2,112]{1,0:T(2,128)S(1)} %bitcast.9), custom_call_target="tpu_custom_call" | custom-call | tf_op jit(solution)/shard_map/pallas_call | solution.py:363
  11.8 1.4 %shard_map.30 = (f32[81,16,128]{2,1,0:T(8,128)S(1)}, f32[81,16,128]{2,1,0:T(8,128)S(1)}, f32[81,16,128]{2,1,0:T(8,128)S(1)}, f32[81,16,128]{2,1,0:T(8,128)S(1)},...) custom-call(s32[1,384]{1,0:T(1,128)S(4)} %get-tuple-element.32.list_, ...), custom_call_target="tpu_custom_call" | custom-call | tf_op jit(solution)/shard_map/pallas_call | solution.py:367
  13.2 4.2 %collective-permute-done.4.cross_ref = bf16[21,16,128]{2,1,0:T(8,128)(2,1)S(1)} collective-permute-done((bf16[21,16,128]{2,1,0:T(8,128)(2,1)S(1)}, bf16[21,16,128]{2,1,0:T(8,128)(2,1)S(1)}, u32[]{:S(2)}, u32[]{:S(2)}) %collective-permute-start.4) | collective-permute-done | bytes 86048 | tf_op jit(solution)/shard_map/ppermute | solution.py:302
  17.4 0.0 collective-permute-done.5.za_ref
  17.4 1.8 %shard_map.31 = (f32[81,16,128]{2,1,0:T(8,128)S(1)}, f32[81,16,128]{2,1,0:T(8,128)S(1)}, f32[81,16,128]{2,1,0:T(8,128)S(1)}, f32[81,16,128]{2,1,0:T(8,128)S(1)},...) custom-call(s32[1,384]{1,0:T(1,128)S(4)} %get-tuple-element.32.list_, ...), custom_call_target="tpu_custom_call", output_to_operand_aliasing={{0}: (6, {}), {1}: (7, {}), {2}: (8, {}), {3}: (9, {}), {4}... | custom-call | tf_op jit(solution)/shard_map/pallas_call | solution.py:375
  19.1 0.0 collective-permute-done.3.zb_ref
  19.2 2.3 %shard_map.32 = (f32[2,10,16,128]{3,2,1,0:T(8,128)}, f32[81,16,128]{2,1,0:T(8,128)S(1)}, f32[81,16,128]{2,1,0:T(8,128)S(1)}, f32[81,16,128]{2,1,0:T(8,128)S(1)},...) custom-call(s32[1,384]{1,0:T(1,128)S(4)} %get-tuple-element.32.list_, ...), custom_call_target="tpu_custom_call", output_to_operand_aliasing={{1}: (7, {}), {2}: (8, {}), {3}: (9, {}), {4}: (10, {}), {5... | custom-call | tf_op jit(solution)/shard_map/pallas_call | solution.py:384
  (2 shorter events, 0.0 us)
Async XLA Ops:
  0.0 4.7 %collective-permute-start.1 = (bf16[20,16,128]{2,1,0:T(8,128)(2,1)}, bf16[20,16,128]{2,1,0:T(8,128)(2,1)S(1)}, u32[]{:S(2)}, u32[]{:S(2)}) collective-permute-start(bf16[20,16,128]{2,1,0:T(8,128)(2,1)} %bitcast.4), channel_id=1, source_target_pairs={{0,2},{4,6},{8,10},{12,14},{2,0},{6,4},{10,8},{14,12},{1,3},{5,7},... | collective-permute-start | bytes 245768 | tf_op jit(solution)/shard_map/ppermute | solution.py:302
  0.0 0.9 %copy-start = (bf16[2,10,16,128]{3,2,1,0:T(8,128)(2,1)S(1)}, bf16[2,10,16,128]{3,2,1,0:T(8,128)(2,1)}, u32[]{:S(2)}) copy-start(bf16[2,10,16,128]{3,2,1,0:T(8,128)(2,1)} %param.2) | copy-start | bytes 245764
  1.0 3.1 %collective-permute-start.2 = (bf16[16,128]{1,0:T(8,128)(2,1)S(1)}, bf16[16,128]{1,0:T(8,128)(2,1)S(1)}, u32[]{:S(2)}, u32[]{:S(2)}) collective-permute-start(bf16[16,128]{1,0:T(8,128)(2,1)S(1)} %get-tuple-element.39), channel_id=1, source_target_pairs={{0,3},{1,2},{4,7},{5,6},{8,11},{9,10},{12,15},{13,14},{3,0},{2,1},... | collective-permute-start | bytes 12296 | tf_op jit(solution)/shard_map/ppermute | solution.py:302
  2.3 1.9 %collective-permute-start = (bf16[16,128]{1,0:T(8,128)(2,1)S(1)}, bf16[16,128]{1,0:T(8,128)(2,1)S(1)}, u32[]{:S(2)}, u32[]{:S(2)}) collective-permute-start(bf16[16,128]{1,0:T(8,128)(2,1)S(1)} %get-tuple-element.39), channel_id=1, source_target_pairs={{0,1},{1,0},{2,3},{3,2},{4,5},{5,4},{6,7},{7,6},{8,9},{9,8},{10,11... | collective-permute-start | bytes 12296 | tf_op jit(solution)/shard_map/ppermute | solution.py:302
  4.7 12.6 %collective-permute-start.5 = (bf16[42,16,128]{2,1,0:T(8,128)(2,1)S(1)}, bf16[42,16,128]{2,1,0:T(8,128)(2,1)S(1)}, u32[]{:S(2)}, u32[]{:S(2)}) collective-permute-start(bf16[42,16,128]{2,1,0:T(8,128)(2,1)S(1)} %pad_maximum_fusion), channel_id=1, source_target_pairs={{0,4},{2,6},{8,12},{10,14},{4,0},{6,2},{12,8},{14,10},{1,5},{3,7},... | collective-permute-start | bytes 516104 | tf_op jit(solution)/shard_map/ppermute | solution.py:302
  6.4 12.8 %collective-permute-start.3 = (bf16[42,16,128]{2,1,0:T(8,128)(2,1)S(1)}, bf16[42,16,128]{2,1,0:T(8,128)(2,1)S(1)}, u32[]{:S(2)}, u32[]{:S(2)}) collective-permute-start(bf16[42,16,128]{2,1,0:T(8,128)(2,1)S(1)} %pad_maximum_fusion), channel_id=1, source_target_pairs={{4,8},{6,10},{0,2},{12,14},{8,4},{10,6},{2,0},{14,12},{5,9},{7,11}... | collective-permute-start | bytes 516104 | tf_op jit(solution)/shard_map/ppermute | solution.py:302
  7.8 9.5 %collective-permute-start.4 = (bf16[21,16,128]{2,1,0:T(8,128)(2,1)S(1)}, bf16[21,16,128]{2,1,0:T(8,128)(2,1)S(1)}, u32[]{:S(2)}, u32[]{:S(2)}) collective-permute-start(bf16[21,16,128]{2,1,0:T(8,128)(2,1)S(1)} %pad_maximum_fusion.1), channel_id=1, source_target_pairs={{2,8},{6,12},{0,4},{10,14},{8,2},{12,6},{4,0},{14,10},{3,9},{7,13}... | collective-permute-start | bytes 258056 | tf_op jit(solution)/shard_map/ppermute | solution.py:302
  9.9 0.7 %copy-start.1 = (s32[112,2]{0,1:T(2,128)S(1)}, s32[112,2]{0,1:T(2,128)}, u32[]{:S(2)}) copy-start(s32[112,2]{0,1:T(2,128)} %param.3) | copy-start | bytes 2692

commit v5 on v4

--- a/solution.py
+++ b/solution.py
@@ -249,9 +249,13 @@
     load = loader(dates, cols, width, boxes, fields)
     others, n2, n3 = counts[0, 2], counts[0, 3], counts[0, 4]
     down = 1 + 4 * far
-    load(zb_ref, 0, zb_ref[tiles - 1], (down + odd) * dates)
-    load(zb_ref, tiles, zb_ref[2 * tiles - 1], (down + 1 - odd) * dates)
-    cohere(boxes, fields, (are, aim), list_i, list_j, cre, cim, late_at, others, batch)
+
+    @pl.when(others > 0)
+    def _():
+        load(zb_ref, 0, zb_ref[tiles - 1], (down + odd) * dates)
+        load(zb_ref, tiles, zb_ref[2 * tiles - 1], (down + 1 - odd) * dates)
+        cohere(boxes, fields, (are, aim), list_i, list_j, cre, cim, late_at, others, batch)
+
 
     def scaled(re, im):
         scale = lax.rsqrt(jnp.maximum(re * re + im * im, 1.0))
@@ -296,9 +300,13 @@
 
 
 def swap(array, axis, matching):
-    matched = {i for pair in matching for i in pair}
-    alone = [i for i in range(lax.axis_size(axis)) if i not in matched]
-    pairing = [*matching, *zip(alone[::2], alone[1::2], strict=True)]
+    pairing = matching
+    if axis == "date":
+        axis, halves = ("date", "pix"), range(2)
+        matched = {i for pair in matching for i in pair}
+        alone = [i for i in range(lax.axis_size("date")) if i not in matched]
+        pairing = [(2 * i + p, 2 * j + p) for i, j in matching for p in halves]
+        pairing += [(2 * i, 2 * i + 1) for i in alone]
     return lax.ppermute(array, axis, [*pairing, *((j, i) for i, j in pairing)])
 
 

time: 21.6 us -> 21.1 us (0.977)
  Pallas kernels: 6.69 us -> 6.21 us
    pallas_call x1, Pallas kernels: 2.26 us -> 1.78 us  [on_device(): pl.pallas_call(functools.partial(link_kernel, batch=batch, unroll=unroll,...]
where the time goes in v5:
time: 21.1 us; the launch traced here: 20.9 us
  starting transfers between devices  7.4 us (35%)
  Pallas kernels  6.21 us (29%)
  waiting for transfers between devices  5.64 us (27%)
  local copies, waits for them, and re-layouts  1.6 us (8%)
    ppermute x6, starting transfers between devices, swap(): return lax.ppermute(array, axis, [*pairing, *((j, i) for i, j in pairing)])  7.4 us
    ppermute x6, waiting for transfers between devices, swap(): return lax.ppermute(array, axis, [*pairing, *((j, i) for i, j in pairing)])  5.64 us
    pallas_call x1, Pallas kernels, on_device(): pl.pallas_call(functools.partial(link_kernel, batch=batch, unroll=unroll,...  1.78 us
    pallas_call x1, Pallas kernels, on_device(): pl.pallas_call(functools.partial(mid_kernel, batch=batch, width=width, da...  1.78 us
    unnamed x4, local copies, waits for them, and re-layouts  1.6 us
    pallas_call x1, Pallas kernels, on_device(): pl.pallas_call(functools.partial(near_kernel, dates=dates, batch=batch, w...  1.37 us
    pallas_call x1, Pallas kernels, on_device(): lists = chosen(pairs.T)  1.18 us
  transfers between devices with their start and end apart: 6, of which 3 were waited for; matrix products, arithmetic and copies ran while one was open for 0% of the time, Pallas kernels for 21%

profile of v5, /device:TPU:4, one launch (start us, length us, event | category | flops | bytes accessed | tf_op | source)
XLA Modules:
  0.0 20.9 jit_solution(1133205241271660806)
XLA Ops:
  0.0 0.0 collective-permute-start.1
  0.0 0.0 copy-start
  0.0 0.9 %copy-done = bf16[2,10,16,128]{3,2,1,0:T(8,128)(2,1)S(1)} copy-done((bf16[2,10,16,128]{3,2,1,0:T(8,128)(2,1)S(1)}, bf16[2,10,16,128]{3,2,1,0:T(8,128)(2,1)}, u32[]{:S(2)}) %copy-start) | copy-done | bytes 81944
  0.9 0.1 shard_map.29
  1.0 1.2 %collective-permute-start.2 = (bf16[16,128]{1,0:T(8,128)(2,1)S(1)}, bf16[16,128]{1,0:T(8,128)(2,1)S(1)}, u32[]{:S(2)}, u32[]{:S(2)}) collective-permute-start(bf16[16,128]{1,0:T(8,128)(2,1)S(1)} %get-tuple-element.39), channel_id=1, source_target_pairs={{0,3},{1,2},{4,7},{5,6},{8,11},{9,10},{12,15},{13,14},{3,0},{2,1},... | collective-permute-start | bytes 12296 | tf_op jit(solution)/shard_map/ppermute | solution.py:310
  2.3 1.0 %collective-permute-start = (bf16[16,128]{1,0:T(8,128)(2,1)S(1)}, bf16[16,128]{1,0:T(8,128)(2,1)S(1)}, u32[]{:S(2)}, u32[]{:S(2)}) collective-permute-start(bf16[16,128]{1,0:T(8,128)(2,1)S(1)} %get-tuple-element.39), channel_id=1, source_target_pairs={{0,1},{1,0},{2,3},{3,2},{4,5},{5,4},{6,7},{7,6},{8,9},{9,8},{10,11... | collective-permute-start | bytes 12296 | tf_op jit(solution)/shard_map/ppermute | solution.py:310
  3.2 0.9 %collective-permute-done.2.edge_mate_ref = bf16[16,128]{1,0:T(8,128)(2,1)S(1)} collective-permute-done((bf16[16,128]{1,0:T(8,128)(2,1)S(1)}, bf16[16,128]{1,0:T(8,128)(2,1)S(1)}, u32[]{:S(2)}, u32[]{:S(2)}) %collective-permute-start.2) | collective-permute-done | bytes 4128 | tf_op jit(solution)/shard_map/ppermute | solution.py:310
  4.2 0.0 collective-permute-done.edge_mine_ref
  4.2 0.5 %collective-permute-done.1.mate_ref = bf16[20,16,128]{2,1,0:T(8,128)(2,1)S(1)} collective-permute-done((bf16[20,16,128]{2,1,0:T(8,128)(2,1)}, bf16[20,16,128]{2,1,0:T(8,128)(2,1)S(1)}, u32[]{:S(2)}, u32[]{:S(2)}) %collective-permute-start.1) | collective-permute-done | bytes 81952 | tf_op jit(solution)/shard_map/ppermute | solution.py:310
  4.7 1.6 %collective-permute-start.5 = (bf16[42,16,128]{2,1,0:T(8,128)(2,1)S(1)}, bf16[42,16,128]{2,1,0:T(8,128)(2,1)S(1)}, u32[]{:S(2)}, u32[]{:S(2)}) collective-permute-start(bf16[42,16,128]{2,1,0:T(8,128)(2,1)S(1)} %pad_maximum_fusion), channel_id=1, source_target_pairs={{0,4},{1,5},{2,6},{3,7},{8,12},{9,13},{10,14},{11,15},{4,0},{5,1},... | collective-permute-start | bytes 516104 | tf_op jit(solution)/shard_map/ppermute | solution.py:310
  6.4 0.0 collective-permute-start.3
  6.4 3.5 %collective-permute-start.4 = (bf16[21,16,128]{2,1,0:T(8,128)(2,1)S(1)}, bf16[21,16,128]{2,1,0:T(8,128)(2,1)S(1)}, u32[]{:S(2)}, u32[]{:S(2)}) collective-permute-start(bf16[21,16,128]{2,1,0:T(8,128)(2,1)S(1)} %pad_maximum_fusion.1), channel_id=1, source_target_pairs={{2,8},{3,9},{6,12},{7,13},{0,1},{4,5},{10,11},{14,15},{8,2},{9,3},... | collective-permute-start | bytes 258056 | tf_op jit(solution)/shard_map/ppermute | solution.py:310
  9.9 0.0 copy-start.1
  9.9 0.7 %copy-done.1 = s32[112,2]{0,1:T(2,128)S(1)} copy-done((s32[112,2]{0,1:T(2,128)S(1)}, s32[112,2]{0,1:T(2,128)}, u32[]{:S(2)}) %copy-start.1) | copy-done | bytes 920
  10.6 1.2 %shard_map.28 = (s32[1,384]{1,0:T(1,128)S(4)}, s32[1,384]{1,0:T(1,128)S(4)}, s32[1,384]{1,0:T(1,128)S(4)}, s32[1,384]{1,0:T(1,128)S(4)}, s32[1,384]{1,0:T(1,128)S(4)}, /*index=5*/bf16[256,128]{1,0:T(8,128)(2,1)S(1)}) custom-call(s32[2,112]{1,0:T(2,128)S(1)} %bitcast.9), custom_call_target="tpu_custom_call" | custom-call | tf_op jit(solution)/shard_map/pallas_call | solution.py:371
  11.8 1.4 %shard_map.30 = (f32[81,16,128]{2,1,0:T(8,128)S(1)}, f32[81,16,128]{2,1,0:T(8,128)S(1)}, f32[81,16,128]{2,1,0:T(8,128)S(1)}, f32[81,16,128]{2,1,0:T(8,128)S(1)},...) custom-call(s32[1,384]{1,0:T(1,128)S(4)} %get-tuple-element.32.list_, ...), custom_call_target="tpu_custom_call" | custom-call | tf_op jit(solution)/shard_map/pallas_call | solution.py:375
  13.2 4.2 %collective-permute-done.4.cross_ref = bf16[21,16,128]{2,1,0:T(8,128)(2,1)S(1)} collective-permute-done((bf16[21,16,128]{2,1,0:T(8,128)(2,1)S(1)}, bf16[21,16,128]{2,1,0:T(8,128)(2,1)S(1)}, u32[]{:S(2)}, u32[]{:S(2)}) %collective-permute-start.4) | collective-permute-done | bytes 86048 | tf_op jit(solution)/shard_map/ppermute | solution.py:310
  17.4 0.0 collective-permute-done.5.za_ref
  17.4 1.8 %shard_map.31 = (f32[81,16,128]{2,1,0:T(8,128)S(1)}, f32[81,16,128]{2,1,0:T(8,128)S(1)}, f32[81,16,128]{2,1,0:T(8,128)S(1)}, f32[81,16,128]{2,1,0:T(8,128)S(1)},...) custom-call(s32[1,384]{1,0:T(1,128)S(4)} %get-tuple-element.32.list_, ...), custom_call_target="tpu_custom_call", output_to_operand_aliasing={{0}: (6, {}), {1}: (7, {}), {2}: (8, {}), {3}: (9, {}), {4}... | custom-call | tf_op jit(solution)/shard_map/pallas_call | solution.py:383
  19.1 0.0 collective-permute-done.3.zb_ref
  19.2 1.8 %shard_map.32 = (f32[2,10,16,128]{3,2,1,0:T(8,128)}, f32[81,16,128]{2,1,0:T(8,128)S(1)}, f32[81,16,128]{2,1,0:T(8,128)S(1)}, f32[81,16,128]{2,1,0:T(8,128)S(1)},...) custom-call(s32[1,384]{1,0:T(1,128)S(4)} %get-tuple-element.32.list_, ...), custom_call_target="tpu_custom_call", output_to_operand_aliasing={{1}: (7, {}), {2}: (8, {}), {3}: (9, {}), {4}: (10, {}), {5... | custom-call | tf_op jit(solution)/shard_map/pallas_call | solution.py:392
  (2 shorter events, 0.0 us)
Async XLA Ops:
  0.0 4.7 %collective-permute-start.1 = (bf16[20,16,128]{2,1,0:T(8,128)(2,1)}, bf16[20,16,128]{2,1,0:T(8,128)(2,1)S(1)}, u32[]{:S(2)}, u32[]{:S(2)}) collective-permute-start(bf16[20,16,128]{2,1,0:T(8,128)(2,1)} %bitcast.4), channel_id=1, source_target_pairs={{0,2},{1,3},{4,6},{5,7},{8,10},{9,11},{12,14},{13,15},{2,0},{3,1},... | collective-permute-start | bytes 245768 | tf_op jit(solution)/shard_map/ppermute | solution.py:310
  0.0 0.9 %copy-start = (bf16[2,10,16,128]{3,2,1,0:T(8,128)(2,1)S(1)}, bf16[2,10,16,128]{3,2,1,0:T(8,128)(2,1)}, u32[]{:S(2)}) copy-start(bf16[2,10,16,128]{3,2,1,0:T(8,128)(2,1)} %param.2) | copy-start | bytes 245764
  1.0 3.1 %collective-permute-start.2 = (bf16[16,128]{1,0:T(8,128)(2,1)S(1)}, bf16[16,128]{1,0:T(8,128)(2,1)S(1)}, u32[]{:S(2)}, u32[]{:S(2)}) collective-permute-start(bf16[16,128]{1,0:T(8,128)(2,1)S(1)} %get-tuple-element.39), channel_id=1, source_target_pairs={{0,3},{1,2},{4,7},{5,6},{8,11},{9,10},{12,15},{13,14},{3,0},{2,1},... | collective-permute-start | bytes 12296 | tf_op jit(solution)/shard_map/ppermute | solution.py:310
  2.3 1.9 %collective-permute-start = (bf16[16,128]{1,0:T(8,128)(2,1)S(1)}, bf16[16,128]{1,0:T(8,128)(2,1)S(1)}, u32[]{:S(2)}, u32[]{:S(2)}) collective-permute-start(bf16[16,128]{1,0:T(8,128)(2,1)S(1)} %get-tuple-element.39), channel_id=1, source_target_pairs={{0,1},{1,0},{2,3},{3,2},{4,5},{5,4},{6,7},{7,6},{8,9},{9,8},{10,11... | collective-permute-start | bytes 12296 | tf_op jit(solution)/shard_map/ppermute | solution.py:310
  4.7 12.6 %collective-permute-start.5 = (bf16[42,16,128]{2,1,0:T(8,128)(2,1)S(1)}, bf16[42,16,128]{2,1,0:T(8,128)(2,1)S(1)}, u32[]{:S(2)}, u32[]{:S(2)}) collective-permute-start(bf16[42,16,128]{2,1,0:T(8,128)(2,1)S(1)} %pad_maximum_fusion), channel_id=1, source_target_pairs={{0,4},{1,5},{2,6},{3,7},{8,12},{9,13},{10,14},{11,15},{4,0},{5,1},... | collective-permute-start | bytes 516104 | tf_op jit(solution)/shard_map/ppermute | solution.py:310
  6.4 12.8 %collective-permute-start.3 = (bf16[42,16,128]{2,1,0:T(8,128)(2,1)S(1)}, bf16[42,16,128]{2,1,0:T(8,128)(2,1)S(1)}, u32[]{:S(2)}, u32[]{:S(2)}) collective-permute-start(bf16[42,16,128]{2,1,0:T(8,128)(2,1)S(1)} %pad_maximum_fusion), channel_id=1, source_target_pairs={{4,8},{5,9},{6,10},{7,11},{0,1},{2,3},{12,13},{14,15},{8,4},{9,5},... | collective-permute-start | bytes 516104 | tf_op jit(solution)/shard_map/ppermute | solution.py:310
  6.4 11.0 %collective-permute-start.4 = (bf16[21,16,128]{2,1,0:T(8,128)(2,1)S(1)}, bf16[21,16,128]{2,1,0:T(8,128)(2,1)S(1)}, u32[]{:S(2)}, u32[]{:S(2)}) collective-permute-start(bf16[21,16,128]{2,1,0:T(8,128)(2,1)S(1)} %pad_maximum_fusion.1), channel_id=1, source_target_pairs={{2,8},{3,9},{6,12},{7,13},{0,1},{4,5},{10,11},{14,15},{8,2},{9,3},... | collective-permute-start | bytes 258056 | tf_op jit(solution)/shard_map/ppermute | solution.py:310
  9.9 0.7 %copy-start.1 = (s32[112,2]{0,1:T(2,128)S(1)}, s32[112,2]{0,1:T(2,128)}, u32[]{:S(2)}) copy-start(s32[112,2]{0,1:T(2,128)} %param.3) | copy-start | bytes 2692

commit v6 on v5

--- a/solution.py
+++ b/solution.py
@@ -254,8 +254,8 @@
     def _():
         load(zb_ref, 0, zb_ref[tiles - 1], (down + odd) * dates)
         load(zb_ref, tiles, zb_ref[2 * tiles - 1], (down + 1 - odd) * dates)
-        cohere(boxes, fields, (are, aim), list_i, list_j, cre, cim, late_at, others, batch)
-
+
+    cohere(boxes, fields, (are, aim), list_i, list_j, cre, cim, late_at, others, batch)
 
     def scaled(re, im):
         scale = lax.rsqrt(jnp.maximum(re * re + im * im, 1.0))
@@ -263,8 +263,8 @@
 
     def settle(low, count, xr, xi, yr, yi):
         def one(q, carry):
-            for u in range(width):
-                w = low + width * q + u
+            for u in range(dates):
+                w = low + dates * q + u
                 re, im = scaled(xr[w], xi[w])
                 xr[w] = re
                 xi[w] = im
@@ -272,7 +272,7 @@
                 yi[w] = im
             return carry
 
-        lax.fori_loop(0, count // width, one, 0)
+        lax.fori_loop(0, count // dates, one, 0)
 
     def step(index, count, xr, xi, yr, yi):
         def several(first):
@@ -345,7 +345,7 @@
     za = swap(both, "date", matching(2, lambda i: i // 2 % 2 == 0))
     zb = swap(both, "date", matching(2, lambda i: i // 2 % 2 == 1))
 
-    unroll = max(1, 128 // rows)
+    unroll = max(1, 256 // rows)
     batch = max(1, 128 // rows)
     width = max(w for w in range(1, 2 * unroll + 1) if dates % w == 0)
     per_block = min(pair_count, 2 * pair_count // size)

time: 21.1 us -> 21.3 us (level)
  Pallas kernels: 6.21 us -> 6.5 us
    pallas_call x1, Pallas kernels: 1.78 us -> 2 us  [on_device(): pl.pallas_call(functools.partial(link_kernel, batch=batch, unroll=unroll,...]
where the time goes in v6:
time: 21.3 us; the launch traced here: 21.2 us
  starting transfers between devices  7.4 us (35%)
  Pallas kernels  6.5 us (31%)
  waiting for transfers between devices  5.58 us (26%)
  local copies, waits for them, and re-layouts  1.6 us (8%)
    ppermute x6, starting transfers between devices, swap(): return lax.ppermute(array, axis, [*pairing, *((j, i) for i, j in pairing)])  7.4 us
    ppermute x6, waiting for transfers between devices, swap(): return lax.ppermute(array, axis, [*pairing, *((j, i) for i, j in pairing)])  5.58 us
    pallas_call x1, Pallas kernels, on_device(): pl.pallas_call(functools.partial(link_kernel, batch=batch, unroll=unroll,...  2 us
    pallas_call x1, Pallas kernels, on_device(): pl.pallas_call(functools.partial(mid_kernel, batch=batch, width=width, da...  1.8 us
    unnamed x4, local copies, waits for them, and re-layouts  1.6 us
    pallas_call x1, Pallas kernels, on_device(): pl.pallas_call(functools.partial(near_kernel, dates=dates, batch=batch, w...  1.38 us
    pallas_call x1, Pallas kernels, on_device(): lists = chosen(pairs.T)  1.22 us
  transfers between devices with their start and end apart: 6, of which 3 were waited for; matrix products, arithmetic and copies ran while one was open for 0% of the time, Pallas kernels for 21%

profile of v6, /device:TPU:4, one launch (start us, length us, event | category | flops | bytes accessed | tf_op | source)
XLA Modules:
  0.0 21.2 jit_solution(8756371663365309695)
XLA Ops:
  0.0 0.0 collective-permute-start.1
  0.0 0.0 copy-start
  0.0 0.9 %copy-done = bf16[2,10,16,128]{3,2,1,0:T(8,128)(2,1)S(1)} copy-done((bf16[2,10,16,128]{3,2,1,0:T(8,128)(2,1)S(1)}, bf16[2,10,16,128]{3,2,1,0:T(8,128)(2,1)}, u32[]{:S(2)}) %copy-start) | copy-done | bytes 81944
  0.9 0.1 shard_map.29
  1.0 1.2 %collective-permute-start.2 = (bf16[16,128]{1,0:T(8,128)(2,1)S(1)}, bf16[16,128]{1,0:T(8,128)(2,1)S(1)}, u32[]{:S(2)}, u32[]{:S(2)}) collective-permute-start(bf16[16,128]{1,0:T(8,128)(2,1)S(1)} %get-tuple-element.39), channel_id=1, source_target_pairs={{0,3},{1,2},{4,7},{5,6},{8,11},{9,10},{12,15},{13,14},{3,0},{2,1},... | collective-permute-start | bytes 12296 | tf_op jit(solution)/shard_map/ppermute | solution.py:310
  2.3 1.0 %collective-permute-start = (bf16[16,128]{1,0:T(8,128)(2,1)S(1)}, bf16[16,128]{1,0:T(8,128)(2,1)S(1)}, u32[]{:S(2)}, u32[]{:S(2)}) collective-permute-start(bf16[16,128]{1,0:T(8,128)(2,1)S(1)} %get-tuple-element.39), channel_id=1, source_target_pairs={{0,1},{1,0},{2,3},{3,2},{4,5},{5,4},{6,7},{7,6},{8,9},{9,8},{10,11... | collective-permute-start | bytes 12296 | tf_op jit(solution)/shard_map/ppermute | solution.py:310
  3.2 0.9 %collective-permute-done.2.edge_mate_ref = bf16[16,128]{1,0:T(8,128)(2,1)S(1)} collective-permute-done((bf16[16,128]{1,0:T(8,128)(2,1)S(1)}, bf16[16,128]{1,0:T(8,128)(2,1)S(1)}, u32[]{:S(2)}, u32[]{:S(2)}) %collective-permute-start.2) | collective-permute-done | bytes 4128 | tf_op jit(solution)/shard_map/ppermute | solution.py:310
  4.2 0.0 collective-permute-done.edge_mine_ref
  4.2 0.5 %collective-permute-done.1.mate_ref = bf16[20,16,128]{2,1,0:T(8,128)(2,1)S(1)} collective-permute-done((bf16[20,16,128]{2,1,0:T(8,128)(2,1)}, bf16[20,16,128]{2,1,0:T(8,128)(2,1)S(1)}, u32[]{:S(2)}, u32[]{:S(2)}) %collective-permute-start.1) | collective-permute-done | bytes 81952 | tf_op jit(solution)/shard_map/ppermute | solution.py:310
  4.7 1.6 %collective-permute-start.5 = (bf16[42,16,128]{2,1,0:T(8,128)(2,1)S(1)}, bf16[42,16,128]{2,1,0:T(8,128)(2,1)S(1)}, u32[]{:S(2)}, u32[]{:S(2)}) collective-permute-start(bf16[42,16,128]{2,1,0:T(8,128)(2,1)S(1)} %pad_maximum_fusion), channel_id=1, source_target_pairs={{0,4},{1,5},{2,6},{3,7},{8,12},{9,13},{10,14},{11,15},{4,0},{5,1},... | collective-permute-start | bytes 516104 | tf_op jit(solution)/shard_map/ppermute | solution.py:310
  6.4 0.0 collective-permute-start.3
  6.4 3.5 %collective-permute-start.4 = (bf16[21,16,128]{2,1,0:T(8,128)(2,1)S(1)}, bf16[21,16,128]{2,1,0:T(8,128)(2,1)S(1)}, u32[]{:S(2)}, u32[]{:S(2)}) collective-permute-start(bf16[21,16,128]{2,1,0:T(8,128)(2,1)S(1)} %pad_maximum_fusion.1), channel_id=1, source_target_pairs={{2,8},{3,9},{6,12},{7,13},{0,1},{4,5},{10,11},{14,15},{8,2},{9,3},... | collective-permute-start | bytes 258056 | tf_op jit(solution)/shard_map/ppermute | solution.py:310
  9.9 0.0 copy-start.1
  9.9 0.7 %copy-done.1 = s32[112,2]{0,1:T(2,128)S(1)} copy-done((s32[112,2]{0,1:T(2,128)S(1)}, s32[112,2]{0,1:T(2,128)}, u32[]{:S(2)}) %copy-start.1) | copy-done | bytes 920
  10.6 1.2 %shard_map.28 = (s32[1,512]{1,0:T(1,128)S(4)}, s32[1,512]{1,0:T(1,128)S(4)}, s32[1,512]{1,0:T(1,128)S(4)}, s32[1,512]{1,0:T(1,128)S(4)}, s32[1,512]{1,0:T(1,128)S(4)}, /*index=5*/bf16[256,128]{1,0:T(8,128)(2,1)S(1)}) custom-call(s32[2,112]{1,0:T(2,128)S(1)} %bitcast.9), custom_call_target="tpu_custom_call" | custom-call | tf_op jit(solution)/shard_map/pallas_call | solution.py:371
  11.8 1.4 %shard_map.30 = (f32[81,16,128]{2,1,0:T(8,128)S(1)}, f32[81,16,128]{2,1,0:T(8,128)S(1)}, f32[81,16,128]{2,1,0:T(8,128)S(1)}, f32[81,16,128]{2,1,0:T(8,128)S(1)},...) custom-call(s32[1,512]{1,0:T(1,128)S(4)} %get-tuple-element.32.list_, ...), custom_call_target="tpu_custom_call" | custom-call | tf_op jit(solution)/shard_map/pallas_call | solution.py:375
  13.2 4.1 %collective-permute-done.4.cross_ref = bf16[21,16,128]{2,1,0:T(8,128)(2,1)S(1)} collective-permute-done((bf16[21,16,128]{2,1,0:T(8,128)(2,1)S(1)}, bf16[21,16,128]{2,1,0:T(8,128)(2,1)S(1)}, u32[]{:S(2)}, u32[]{:S(2)}) %collective-permute-start.4) | collective-permute-done | bytes 86048 | tf_op jit(solution)/shard_map/ppermute | solution.py:310
  17.4 0.0 collective-permute-done.5.za_ref
  17.4 1.8 %shard_map.31 = (f32[81,16,128]{2,1,0:T(8,128)S(1)}, f32[81,16,128]{2,1,0:T(8,128)S(1)}, f32[81,16,128]{2,1,0:T(8,128)S(1)}, f32[81,16,128]{2,1,0:T(8,128)S(1)},...) custom-call(s32[1,512]{1,0:T(1,128)S(4)} %get-tuple-element.32.list_, ...), custom_call_target="tpu_custom_call", output_to_operand_aliasing={{0}: (6, {}), {1}: (7, {}), {2}: (8, {}), {3}: (9, {}), {4}... | custom-call | tf_op jit(solution)/shard_map/pallas_call | solution.py:383
  19.2 0.0 collective-permute-done.3.zb_ref
  19.2 2.0 %shard_map.32 = (f32[2,10,16,128]{3,2,1,0:T(8,128)}, f32[81,16,128]{2,1,0:T(8,128)S(1)}, f32[81,16,128]{2,1,0:T(8,128)S(1)}, f32[81,16,128]{2,1,0:T(8,128)S(1)},...) custom-call(s32[1,512]{1,0:T(1,128)S(4)} %get-tuple-element.32.list_, ...), custom_call_target="tpu_custom_call", output_to_operand_aliasing={{1}: (7, {}), {2}: (8, {}), {3}: (9, {}), {4}: (10, {}), {5... | custom-call | tf_op jit(solution)/shard_map/pallas_call | solution.py:392
  (2 shorter events, 0.0 us)
Async XLA Ops:
  0.0 4.7 %collective-permute-start.1 = (bf16[20,16,128]{2,1,0:T(8,128)(2,1)}, bf16[20,16,128]{2,1,0:T(8,128)(2,1)S(1)}, u32[]{:S(2)}, u32[]{:S(2)}) collective-permute-start(bf16[20,16,128]{2,1,0:T(8,128)(2,1)} %bitcast.4), channel_id=1, source_target_pairs={{0,2},{1,3},{4,6},{5,7},{8,10},{9,11},{12,14},{13,15},{2,0},{3,1},... | collective-permute-start | bytes 245768 | tf_op jit(solution)/shard_map/ppermute | solution.py:310
  0.0 0.9 %copy-start = (bf16[2,10,16,128]{3,2,1,0:T(8,128)(2,1)S(1)}, bf16[2,10,16,128]{3,2,1,0:T(8,128)(2,1)}, u32[]{:S(2)}) copy-start(bf16[2,10,16,128]{3,2,1,0:T(8,128)(2,1)} %param.2) | copy-start | bytes 245764
  1.0 3.1 %collective-permute-start.2 = (bf16[16,128]{1,0:T(8,128)(2,1)S(1)}, bf16[16,128]{1,0:T(8,128)(2,1)S(1)}, u32[]{:S(2)}, u32[]{:S(2)}) collective-permute-start(bf16[16,128]{1,0:T(8,128)(2,1)S(1)} %get-tuple-element.39), channel_id=1, source_target_pairs={{0,3},{1,2},{4,7},{5,6},{8,11},{9,10},{12,15},{13,14},{3,0},{2,1},... | collective-permute-start | bytes 12296 | tf_op jit(solution)/shard_map/ppermute | solution.py:310
  2.3 1.9 %collective-permute-start = (bf16[16,128]{1,0:T(8,128)(2,1)S(1)}, bf16[16,128]{1,0:T(8,128)(2,1)S(1)}, u32[]{:S(2)}, u32[]{:S(2)}) collective-permute-start(bf16[16,128]{1,0:T(8,128)(2,1)S(1)} %get-tuple-element.39), channel_id=1, source_target_pairs={{0,1},{1,0},{2,3},{3,2},{4,5},{5,4},{6,7},{7,6},{8,9},{9,8},{10,11... | collective-permute-start | bytes 12296 | tf_op jit(solution)/shard_map/ppermute | solution.py:310
  4.7 12.6 %collective-permute-start.5 = (bf16[42,16,128]{2,1,0:T(8,128)(2,1)S(1)}, bf16[42,16,128]{2,1,0:T(8,128)(2,1)S(1)}, u32[]{:S(2)}, u32[]{:S(2)}) collective-permute-start(bf16[42,16,128]{2,1,0:T(8,128)(2,1)S(1)} %pad_maximum_fusion), channel_id=1, source_target_pairs={{0,4},{1,5},{2,6},{3,7},{8,12},{9,13},{10,14},{11,15},{4,0},{5,1},... | collective-permute-start | bytes 516104 | tf_op jit(solution)/shard_map/ppermute | solution.py:310
  6.4 12.8 %collective-permute-start.3 = (bf16[42,16,128]{2,1,0:T(8,128)(2,1)S(1)}, bf16[42,16,128]{2,1,0:T(8,128)(2,1)S(1)}, u32[]{:S(2)}, u32[]{:S(2)}) collective-permute-start(bf16[42,16,128]{2,1,0:T(8,128)(2,1)S(1)} %pad_maximum_fusion), channel_id=1, source_target_pairs={{4,8},{5,9},{6,10},{7,11},{0,1},{2,3},{12,13},{14,15},{8,4},{9,5},... | collective-permute-start | bytes 516104 | tf_op jit(solution)/shard_map/ppermute | solution.py:310
  6.4 11.0 %collective-permute-start.4 = (bf16[21,16,128]{2,1,0:T(8,128)(2,1)S(1)}, bf16[21,16,128]{2,1,0:T(8,128)(2,1)S(1)}, u32[]{:S(2)}, u32[]{:S(2)}) collective-permute-start(bf16[21,16,128]{2,1,0:T(8,128)(2,1)S(1)} %pad_maximum_fusion.1), channel_id=1, source_target_pairs={{2,8},{3,9},{6,12},{7,13},{0,1},{4,5},{10,11},{14,15},{8,2},{9,3},... | collective-permute-start | bytes 258056 | tf_op jit(solution)/shard_map/ppermute | solution.py:310
  9.9 0.7 %copy-start.1 = (s32[112,2]{0,1:T(2,128)S(1)}, s32[112,2]{0,1:T(2,128)}, u32[]{:S(2)}) copy-start(s32[112,2]{0,1:T(2,128)} %param.3) | copy-start | bytes 2692
